TPU v7x, 256 devices: a whole 4x4x8 slice. The times are simulated.
256 devices in a mesh: seq: 64 (over y, z, core), head: 4 (over x).
Axes of the slice: x: 4, y: 4, z: 8, core: 2. Of those that a mesh axis runs over, the one named last changes fastest.
Arguments:
- queries: bfloat16 [16384, 32, 128], P('seq', 'head'), may hold values from -16 to 16
- keys: bfloat16 [16384, 32, 128], P('seq', 'head'), may hold values from -40 to 40
- values: bfloat16 [16384, 32, 128], P('seq', 'head'), may hold values from -6 to 6
- cluster_ids: int32 [16384, 32], P('seq', 'head'), may hold values from 0 to 511, as said below
- out_weight: bfloat16 [4096, 4096], P('seq', 'head'), may hold values from -0.09375 to 0.09375
Outputs:
- mixed: bfloat16 [16384, 4096], P('seq', 'head')
Inputs may be any that keep to these rules, and one draw needn't show every extreme that they name: `cluster_ids`: in each head h, the ids j with j % 16 equal to one residue, drawn from the seed for that head, are never used.
All inputs are finite; a program needn't handle non-finite values.
Results may differ from a plain program's by a relative error of at most 0.008.
The roundings to bfloat16 on the way count: a program that leaves them out, or rounds other values in their place, can miss the bound.
Values may be sent and summed in bfloat16 or wider, within the bound.
A program may use at most 320 MiB of HBM per device.

v0:
```python
import math

import jax
import jax.numpy as jnp
from jax import lax
from jax.sharding import PartitionSpec as P

C = 512


def merged_2(part, axis, combine):
    gathered = jax.tree.map(lambda a: lax.all_gather(a, axis), part)

    def take(source):
        return jax.tree.map(lambda a: lax.dynamic_index_in_dim(a, source, 0, False), gathered)

    return lax.fori_loop(
        1, lax.axis_size(axis), lambda source, state: combine(state, take(source)), take(0)
    )


def combine_parts(first, second):
    max_first, total_first, out_first = first
    max_second, total_second, out_second = second
    larger = jnp.maximum(max_first, max_second)
    factor_first = jnp.exp(max_first - larger)
    factor_second = jnp.exp(max_second - larger)
    total = total_first * factor_first + total_second * factor_second
    merged = out_first * factor_first[:, :, None] + out_second * factor_second[:, :, None]
    return (larger, total, merged)


def on_device(queries, keys, values, cluster_ids, out_weight):
    tok_rows, head_count, e_width = queries.shape
    score_scale = 1.0 / math.sqrt(e_width)
    labels = lax.broadcasted_iota(jnp.int32, (head_count, tok_rows, C), 2)
    onehot = (cluster_ids.T[:, :, None] == labels).astype(jnp.bfloat16)
    totals = jnp.einsum("htc,the->hce", onehot, queries, preferred_element_type=jnp.float32)
    counts = jnp.sum(onehot, axis=1, dtype=jnp.float32)
    all_totals, all_counts = lax.psum((totals, counts), "seq")
    centroid = (all_totals / jnp.maximum(all_counts, 1.0)[:, :, None]).astype(jnp.bfloat16)
    scores = (
        jnp.einsum("hce,the->hct", centroid, keys, preferred_element_type=jnp.float32) * score_scale
    )
    local_max = jnp.max(scores, axis=2)
    weights = jnp.exp(scores - local_max[:, :, None])
    local_total = jnp.sum(weights, axis=2)
    local_out = jnp.einsum(
        "hct,the->hce", weights.astype(jnp.bfloat16), values, preferred_element_type=jnp.float32
    )
    merged_max, merged_total, merged_out = merged_2(
        (local_max, local_total, local_out), "seq", combine_parts
    )
    attended = (merged_out / merged_total[:, :, None]).astype(jnp.bfloat16)
    expanded = jnp.einsum(
        "htc,hce->the", onehot, attended, preferred_element_type=jnp.float32
    ).astype(jnp.bfloat16)
    flat = expanded.reshape(tok_rows, head_count * e_width)
    features = lax.all_gather(flat, "head", axis=1, tiled=True)
    mixed = jnp.dot(
        features,
        lax.all_gather(out_weight, "seq", axis=0, tiled=True),
        preferred_element_type=jnp.float32,
    )
    return mixed.astype(jnp.bfloat16)


def solution(mesh):
    placed = (
        P("seq", "head", None),
        P("seq", "head", None),
        P("seq", "head", None),
        P("seq", "head"),
        P("seq", "head"),
    )
    return jax.shard_map(
        on_device, mesh=mesh, in_specs=placed, out_specs=P("seq", "head"), check_vma=False
    )
```

profile of v0, /device:TPU:1, one launch (start us, length us, event | category | flops | bytes accessed | tf_op | source)
XLA Modules:
  0.0 1128.4 jit_solution(14413670766641711489)
XLA Ops:
  6.5 4.0 fusion.5
  11.3 250.1 %psum.15 = f32[8,512]{1,0:T(8,128)S(1)} all-reduce(f32[8,512]{1,0:T(8,128)S(1)} %convert_reduce_fusion), channel_id=1, replica_groups=mesh['seq'=64,'head'=4] {'seq'}, use_global_device_ids=true, to_apply=%region_2.0 | all-reduce | flops 4096 | bytes 32768 | tf_op jit(solution)/shard_map/psum | solution.py:40
  261.3 4.4 multiply_reduce_fusion
  265.7 3.6 fusion.7
  270.1 4.6 fusion.8
  275.4 69.8 %all-gather.15.cloned.1.call-done = f32[512,512]{1,0:T(8,128)} async-done(((f32[8,512]{1,0:T(8,128)}), f32[512,512]{1,0:T(8,128)}) %all-gather.15.cloned.1.call-update) | async-done | bytes 1048592 | tf_op jit(solution)/shard_map/all_gather | solution.py:12
  345.9 76.7 %all-gather.13.cloned.1.call-done = f32[512,512]{1,0:T(8,128)} async-done(((f32[8,512]{1,0:T(8,128)}), f32[512,512]{1,0:T(8,128)}) %all-gather.13.cloned.1.call-update) | async-done | bytes 1048592 | tf_op jit(solution)/shard_map/all_gather | solution.py:12
  423.3 436.1 %all-gather.17.cloned.1.call-done = f32[512,512,128]{2,1,0:T(8,128)} async-done(((f32[8,512,128]{2,1,0:T(8,128)}), f32[512,512,128]{2,1,0:T(8,128)}) %all-gather.17.cloned.1.call-update) | async-done | bytes 134217744 | tf_op jit(solution)/shard_map/all_gather | solution.py:12
  861.1 220.9 %while.19 = (s32[]{:T(128)}, f32[8,512]{1,0:T(8,128)S(1)}, f32[8,512]{1,0:T(8,128)S(1)}, f32[8,512,128]{2,1,0:T(8,128)S(1)}, f32[64,8,512]{2,1,0:T(8,128)}, /*in...) while((s32[]{:T(128)}, f32[8,512]{1,0:T(8,128)S(1)}, ...), condition=%wide.region_6.7_spmd, body=%wide.region_5.6_spmd.sunk | while | flops 1597445 | bytes 6455447 | solution.py:17
  872.4 2.7 fusion.27
  875.9 2.7 fusion.27
  879.4 2.7 fusion.27
  907.4 2.9 fusion.27
  914.6 2.7 fusion.27
  918.1 2.7 fusion.27
  925.1 2.7 fusion.27
  928.6 2.7 fusion.27
  932.2 2.8 fusion.27
  935.7 2.7 fusion.27
  939.3 2.7 fusion.27
  942.8 2.7 fusion.27
  946.3 2.7 fusion.27
  949.8 2.7 fusion.27
  953.3 2.7 fusion.27
  956.8 2.7 fusion.27
  960.3 2.7 fusion.27
  963.8 2.7 fusion.27
  967.3 2.7 fusion.27
  970.8 2.7 fusion.27
  974.3 2.7 fusion.27
  977.8 2.7 fusion.27
  981.3 2.7 fusion.27
  984.8 2.7 fusion.27
  988.3 2.7 fusion.27
  991.8 2.7 fusion.27
  995.3 2.7 fusion.27
  998.8 2.7 fusion.27
  1002.3 2.7 fusion.27
  1005.8 2.7 fusion.27
  1009.3 2.7 fusion.27
  1012.8 2.7 fusion.27
  1016.3 2.7 fusion.27
  1019.8 2.7 fusion.27
  1023.3 2.7 fusion.27
  1026.8 2.7 fusion.27
  1030.3 2.7 fusion.27
  1084.8 29.6 %all-gather.9.cloned.1.call-done = bf16[256,4096]{0,1:T(8,128)(2,1)} async-done(((bf16[256,1024]{0,1:T(8,128)(2,1)}), bf16[256,4096]{0,1:T(8,128)(2,1)}) %all-gather.9.cloned.1.call-update) | async-done | bytes 2097168 | tf_op jit(solution)/shard_map/all_gather | solution.py:59
  1114.4 7.2 convolution_convert_fusion
  (117 shorter events, 126.4 us)
Async XLA Ops:
  6.5 254.8 %copy-start = (bf16[256,8,128]{2,1,0:T(8,128)(2,1)S(1)}, bf16[256,8,128]{2,1,0:T(8,128)(2,1)}, u32[]{:S(2)}) copy-start(bf16[256,8,128]{2,1,0:T(8,128)(2,1)} %param.8) | copy-start | bytes 1572868
  6.5 254.8 %all-reduce.2.cloned.1.call-start = ((), (), s32[]{:S(2)}) async-start(), calls=%async_computation | async-start | bytes 4194304 | tf_op jit(solution)/shard_map/psum | solution.py:40
  6.5 4.1 copy-start.3
  10.6 334.6 %all-gather.15.cloned.1.call-start = ((), (), s32[]{:S(2)}) async-start(), calls=%async_computation.4 | async-start | bytes 1064960 | tf_op jit(solution)/shard_map/all_gather | solution.py:12
  265.7 3.6 copy-start.2
  265.7 4.4 copy-start.1
  269.3 153.3 %all-gather.13.cloned.1.call-start = ((), (), s32[]{:S(2)}) async-start(), calls=%async_computation.3 | async-start | bytes 1064960 | tf_op jit(solution)/shard_map/all_gather | solution.py:12
  270.0 589.3 %all-gather.17.cloned.1.call-start = ((), (), s32[]{:S(2)}) async-start(), calls=%async_computation.5 | async-start | bytes 136314880 | tf_op jit(solution)/shard_map/all_gather | solution.py:12
  274.8 810.0 %all-gather.11.cloned.1.call-start = ((), (), s32[]{:S(2)}) async-start(), calls=%async_computation.2 | async-start | bytes 8519680 | tf_op jit(solution)/shard_map/all_gather | solution.py:62
  275.3 839.0 %all-gather.9.cloned.1.call-start = ((), (), s32[]{:S(2)}) async-start(), calls=%async_computation.1 | async-start | bytes 2621440 | tf_op jit(solution)/shard_map/all_gather | solution.py:59
Sparse Core Ops, SparseCore 0:
  10.8 192.6 all-reduce.1
  269.4 75.7 all-gather.14
  348.0 74.5 all-gather.12
  425.2 434.0 all-gather.16
  862.0 79.9 all-gather.10
  1084.8 29.4 all-gather.8
where the time goes:
time: 1140 us; the launch traced here: 1130 us
  waiting for transfers between devices  613 us (54%)
  blocking collectives  250 us (22%)
  other arithmetic  223 us (20%)
  matrix products  22.9 us (2%)
  between operations  13.5 us (1%)
    all_gather x3, waiting for transfers between devices, merged_2(): gathered = jax.tree.map(lambda a: lax.all_gather(a, axis), part)  583 us
    psum x1, blocking collectives, on_device(): all_totals, all_counts = lax.psum((totals, counts), 'seq')  250 us
    add x63, other arithmetic, combine_parts(): out_first * factor_first[:, :, None]  171 us
    add x63, other arithmetic, combine_parts(): total = total_first * factor_first + total_second * factor_second  47.9 us
    all_gather x1, waiting for transfers between devices, on_device(): features = lax.all_gather(flat, 'head', axis=1, tiled=True)  29.6 us
  transfers between devices with their start and end apart: 6, of which 4 were waited for; matrix products, arithmetic and copies ran while one was open for 20% of the time, Pallas kernels for 0%

commit v1 on v0

v1 whole, which is shorter than its diff:
```python
import math

import jax
import jax.numpy as jnp
from jax import lax
from jax.experimental import pallas as pl
from jax.experimental.pallas import tpu as pltpu
from jax.sharding import PartitionSpec as P

C = 512
E = 128
NY, NZ, NX = 4, 8, 4
TOK = 256
BLK = C // NZ
ROWS = BLK + 8
EXP2_SCALE = math.log2(math.e) / math.sqrt(E)
F32, BF16 = jnp.float32, jnp.bfloat16


def chain_kernel(
    q_ref, k_ref, v_ref, ids_ref, idx_ref, out_ref,
    qbuf, kbuf, vbuf, idbuf, idxbuf, acc, msg, recv_t, recv_o, cent, sbuf, mx, ls,
    att, idcol, fsend, frecv,
    ssem, rq, rk, rv, rid, ridx, rt, rc, ro, rz, ra, rb, rf, lsem,
):
    s_id, x = lax.axis_index("seq"), lax.axis_index("head")
    c = lax.rem(s_id, 2)
    z = lax.rem(lax.div(s_id, 2), NZ)
    y = lax.div(s_id, 2 * NZ)
    yc = y * 2 + c
    g0 = x * NY + y

    def seq_of(yy, zz, cc):
        return (yy * NZ + zz) * 2 + cc

    sends = []

    def put(src, dst, rsem, seq, head):
        cp = pltpu.make_async_remote_copy(
            src_ref=src, dst_ref=dst, send_sem=ssem.at[len(sends)], recv_sem=rsem,
            device_id=(seq, head), device_id_type=pl.DeviceIdType.MESH,
        )
        cp.start()
        sends.append(cp)
        return cp

    def arrived(ref, rsem):
        pltpu.make_async_copy(ref, ref, rsem).wait()

    def yc_peer(d):
        t = lax.rem(yc + d, 8)
        return lax.div(t, 2), lax.rem(t, 2)

    barrier = pltpu.get_barrier_semaphore()

    def greet(seq, head):
        pl.semaphore_signal(barrier, inc=1, device_id=(seq, head), device_id_type=pl.DeviceIdType.MESH)

    for d in range(1, 8):
        ty, tc = yc_peer(d)
        greet(seq_of(ty, z, tc), x)
        greet(seq_of(y, lax.rem(z + d, NZ), c), x)
    for e in range(1, NX):
        greet(s_id, lax.rem(x + e, NX))
        greet(seq_of(y, z, 1 - c), lax.rem(x + e, NX))

    local = []
    own_h = c * NY + y
    for n, (src, dst) in enumerate(
        ((ids_ref.at[own_h], idbuf.at[yc]), (q_ref.at[own_h], qbuf.at[yc]),
         (k_ref.at[own_h], kbuf.at[yc]), (v_ref.at[own_h], vbuf.at[yc]),
         (idx_ref.at[c], idxbuf.at[c]))
    ):
        cp = pltpu.make_async_copy(src, dst, lsem.at[n])
        cp.start()
        local.append(cp)

    pl.semaphore_wait(barrier, 20)

    for src, buf, sem in ((ids_ref, idbuf, rid), (q_ref, qbuf, rq)):
        for d in range(1, 8):
            ty, tc = yc_peer(d)
            put(src.at[tc * NY + ty], buf.at[yc], sem.at[d - 1], seq_of(ty, z, tc), x)
    put(idx_ref.at[1 - c], idxbuf.at[c], ridx.at[1], seq_of(y, z, 1 - c), x)
    for e in range(1, NX):
        for f in range(2):
            tc = lax.rem(c + f, 2)
            put(idx_ref.at[tc], idxbuf.at[(NX - e) * 2 + c], ridx.at[(NX - e) * 2 + f],
                seq_of(y, z, tc), lax.rem(x + e, NX))
    for src, buf, sem in ((k_ref, kbuf, rk), (v_ref, vbuf, rv)):
        for d in range(1, 8):
            ty, tc = yc_peer(d)
            put(src.at[tc * NY + ty], buf.at[yc], sem.at[d - 1], seq_of(ty, z, tc), x)

    def take8(buf, sem):
        for d in range(1, 8):
            arrived(buf.at[lax.rem(yc + 8 - d, 8)], sem.at[d - 1])

    eye = lax.broadcasted_iota(jnp.int32, (BLK, E), 0) == lax.broadcasted_iota(jnp.int32, (BLK, E), 1)

    def to_row(col):
        return jnp.sum(jnp.where(eye, col, 0.0), axis=0, keepdims=True)

    def to_col(row):
        return jnp.sum(jnp.where(eye, row, 0.0), axis=1, keepdims=True)

    local[0].wait()
    local[1].wait()
    take8(idbuf, rid)
    take8(qbuf, rq)
    acc[...] = jnp.zeros_like(acc)

    @pl.loop(0, 8)
    def _(i):
        label = lax.broadcasted_iota(jnp.int32, (C, TOK), 0)
        onehot = (label == idbuf[i]).astype(F32).astype(BF16)
        rhs = jnp.concatenate([qbuf[i], jnp.ones((TOK, E), BF16)], axis=1)
        acc[...] += jnp.dot(onehot, rhs, preferred_element_type=F32)

    @pl.loop(0, NZ)
    def _(b):
        rows = pl.ds(pl.multiple_of(b * BLK, BLK), BLK)
        msg[b, pl.ds(0, BLK), :] = acc[rows, pl.ds(0, E)]
        row = to_row(acc[rows, pl.ds(E, E)])
        msg[b, pl.ds(BLK, 8), :] = jnp.broadcast_to(row, (8, E))

    def reduce_z(recv, sem, src):
        for d in range(1, NZ):
            tz = lax.rem(z + d, NZ)
            put(src.at[tz], recv.at[d - 1], sem.at[d - 1], seq_of(y, tz, c), x)

    reduce_z(recv_t, rt, msg.at[pl.ds(0, NZ)])

    local[4].wait()
    for j in range(1, 8):
        e, f = j // 2, j % 2
        arrived(idxbuf.at[e * 2 + lax.rem(c + f, 2)], ridx.at[j])
    for half in range(2):
        rows = jnp.concatenate([idxbuf[e * 2 + half] for e in range(NX)], axis=0).astype(F32)
        rows = jnp.concatenate([rows, jnp.zeros((E - 8 * NX, TOK), F32)], axis=0)
        idcol[pl.ds(half * TOK, TOK), :] = rows.T

    total = msg[z]
    for d in range(1, NZ):
        arrived(recv_t.at[d - 1], rt.at[d - 1])
        total = total + recv_t[d - 1]
    count = to_col(total[BLK:BLK + 1, :])
    cent[z] = (total[:BLK, :] / jnp.maximum(count, 1.0)).astype(BF16)

    def gather_z(buf, sem):
        for d in range(1, NZ):
            tz = lax.rem(z + d, NZ)
            put(buf.at[z], buf.at[z], sem.at[d - 1], seq_of(y, tz, c), x)

    gather_z(cent, rc)
    local[2].wait()
    take8(kbuf, rk)
    for d in range(1, NZ):
        arrived(cent.at[lax.rem(z + NZ - d, NZ)], rc.at[d - 1])

    centroid = cent[...].reshape(C, E)
    mx[...] = jnp.full_like(mx, -jnp.inf)

    @pl.loop(0, 8)
    def _(i):
        s = lax.dot_general(centroid, kbuf[i], (((1,), (1,)), ((), ())), preferred_element_type=F32)
        sbuf[i] = s
        mx[...] = jnp.maximum(mx[...], jnp.maximum(s[:, :E], s[:, E:]))

    top = jnp.broadcast_to(jnp.max(mx[...], axis=1, keepdims=True), (C, E))
    mx[...] = top
    ls[...] = jnp.zeros_like(ls)
    acc[:, pl.ds(0, E)] = jnp.zeros((C, E), F32)
    local[3].wait()
    take8(vbuf, rv)

    @pl.loop(0, 8)
    def _(i):
        m = mx[...]
        p = jnp.exp2((sbuf[i] - jnp.concatenate([m, m], axis=1)) * EXP2_SCALE)
        ls[...] += p[:, :E] + p[:, E:]
        acc[:, pl.ds(0, E)] += jnp.dot(p.astype(BF16), vbuf[i], preferred_element_type=F32)

    ls[...] = jnp.broadcast_to(jnp.sum(ls[...], axis=1, keepdims=True), (C, E))

    @pl.loop(0, NZ)
    def _(b):
        rows = pl.ds(pl.multiple_of(b * BLK, BLK), BLK)
        msg[NZ + b, pl.ds(0, BLK), :] = acc[rows, pl.ds(0, E)]
        first = lax.broadcasted_iota(jnp.int32, (8, E), 0) == 0
        msg[NZ + b, pl.ds(BLK, 8), :] = jnp.where(first, to_row(mx[rows, :]), to_row(ls[rows, :]))

    reduce_z(recv_o, ro, msg.at[pl.ds(NZ, NZ)])
    parts = [msg[NZ + z]]
    for d in range(1, NZ):
        arrived(recv_o.at[d - 1], ro.at[d - 1])
        parts.append(recv_o[d - 1])
    tops = [to_col(part[BLK:BLK + 1, :]) for part in parts]
    largest = tops[0]
    for t in tops[1:]:
        largest = jnp.maximum(largest, t)
    num, den = 0.0, 0.0
    for part, t in zip(parts, tops):
        factor = jnp.exp2((t - largest) * EXP2_SCALE)
        num = num + part[:BLK, :] * factor
        den = den + to_col(part[BLK + 1:BLK + 2, :]) * factor
    att[g0, z] = (num / den).astype(BF16)

    for d in range(1, NZ):
        tz = lax.rem(z + d, NZ)
        put(att.at[g0, z], att.at[g0, z], rz.at[d - 1], seq_of(y, tz, c), x)
    for d in range(1, NZ):
        arrived(att.at[g0, lax.rem(z + NZ - d, NZ)], rz.at[d - 1])

    low, high = pl.ds(0, NZ // 2), pl.ds(NZ // 2, NZ // 2)

    def g_of(dx, dy):
        return lax.rem(x + dx, NX) * NY + lax.rem(y + dy, NY)

    def to_y(g, part, sem, dx):
        for e in range(1, NY):
            put(att.at[g, part], att.at[g, part], sem.at[dx * NY + NY - e],
                seq_of(lax.rem(y + e, NY), z, c), x)

    def to_x(g, part, sem, dy):
        for e in range(1, NX):
            put(att.at[g, part], att.at[g, part], sem.at[(NX - e) * NY + dy],
                s_id, lax.rem(x + e, NX))

    to_y(g0, low, ra, 0)
    to_x(g0, high, rb, 0)
    to_x(g0, low, ra, 0)
    to_y(g0, high, rb, 0)
    for e in range(1, NY):
        arrived(att.at[g_of(0, e), low], ra.at[e])
        to_x(g_of(0, e), low, ra, e)
        arrived(att.at[g_of(e, 0), high], rb.at[e * NY])
        to_y(g_of(e, 0), high, rb, e)

    lanes = lax.broadcasted_iota(jnp.int32, (2 * TOK, C), 1).astype(F32)
    own = pl.ds(pl.multiple_of(c * TOK, TOK), TOK)
    fcopies = []
    for dx in range(NX):
        xs = lax.rem(x + dx, NX)
        for dy in range(NY):
            g = g_of(dx, dy)
            if dx > 0:
                arrived(att.at[g, low], ra.at[dx * NY + dy])
            if dy > 0:
                arrived(att.at[g, high], rb.at[dx * NY + dy])
            col = idcol[:, pl.ds(dx * 8 + dy, 1)]
            onehot = (lanes == col).astype(F32).astype(BF16)
            feat = jnp.dot(onehot, att[g].reshape(C, E), preferred_element_type=F32).astype(BF16)
            acc_rows = pl.ds(pl.multiple_of((xs * 8 + c * NY + lax.rem(y + dy, NY)) * E, E), E)
            send_cols = pl.ds(pl.multiple_of(g * E, E), E)
            mine = jnp.where(c == 0, feat[:TOK], feat[TOK:])
            theirs = jnp.where(c == 0, feat[TOK:], feat[:TOK])
            out_ref[:, acc_rows] = mine
            fsend[:, send_cols] = theirs
        cols = pl.ds(pl.multiple_of(xs * NY * E, NY * E), NY * E)
        put(fsend.at[:, cols], frecv.at[:, cols], rf.at[dx], seq_of(y, z, 1 - c), x)
    for dx in range(NX):
        xs = lax.rem(x + dx, NX)
        cols = pl.ds(pl.multiple_of(xs * NY * E, NY * E), NY * E)
        arrived(frecv.at[:, cols], rf.at[dx])
        there = pl.ds(pl.multiple_of(xs * 8 * E + (1 - c) * NY * E, NY * E), NY * E)
        out_ref[:, there] = frecv[:, cols]
    for cp in sends:
        cp.wait_send()


def chain(queries, keys, values, ids, idx):
    vmem = pl.BlockSpec(memory_space=pltpu.VMEM)
    anyw = pl.BlockSpec(memory_space=pl.ANY)
    dma = pltpu.SemaphoreType.DMA
    return pl.pallas_call(
        chain_kernel,
        out_shape=jax.ShapeDtypeStruct((TOK, 32 * E), BF16),
        in_specs=[anyw, anyw, anyw, vmem, vmem],
        out_specs=vmem,
        scratch_shapes=[
            pltpu.VMEM((8, TOK, E), BF16), pltpu.VMEM((8, TOK, E), BF16), pltpu.VMEM((8, TOK, E), BF16),
            pltpu.VMEM((8, 1, TOK), jnp.int32), pltpu.VMEM((8, 8, TOK), jnp.int32),
            pltpu.VMEM((C, 2 * E), F32), pltpu.VMEM((2 * NZ, ROWS, E), F32),
            pltpu.VMEM((NZ - 1, ROWS, E), F32), pltpu.VMEM((NZ - 1, ROWS, E), F32),
            pltpu.VMEM((NZ, BLK, E), BF16), pltpu.VMEM((8, C, TOK), F32),
            pltpu.VMEM((C, E), F32), pltpu.VMEM((C, E), F32),
            pltpu.VMEM((16, NZ, BLK, E), BF16), pltpu.VMEM((2 * TOK, E), F32),
            pltpu.VMEM((TOK, 16 * E), BF16), pltpu.VMEM((TOK, 16 * E), BF16),
            dma((112,)), dma((7,)), dma((7,)), dma((7,)), dma((7,)), dma((8,)), dma((7,)), dma((7,)),
            dma((7,)), dma((7,)), dma((16,)), dma((16,)), dma((4,)), dma((5,)),
        ],
        compiler_params=pltpu.CompilerParams(
            collective_id=0, has_side_effects=True, vmem_limit_bytes=48 * 1024 * 1024
        ),
        cost_estimate=pl.CostEstimate(flops=4_000_000_000, bytes_accessed=200_000_000, transcendentals=1 << 20),
    )(queries, keys, values, ids, idx)


def on_device(queries, keys, values, cluster_ids, out_weight):
    y = lax.div(lax.axis_index("seq"), 2 * NZ)
    ids = cluster_ids.T
    pair = ids.reshape(2, NY, TOK)
    pair = lax.dynamic_slice_in_dim(jnp.concatenate([pair, pair], axis=1), y, NY, axis=1)
    idx = jnp.concatenate([pair, jnp.zeros_like(pair)], axis=1)
    weight = lax.all_gather(out_weight, "seq", axis=0, tiled=True)
    q, k, v = (jnp.transpose(a, (1, 0, 2)) for a in (queries, keys, values))
    features = chain(q, k, v, ids[:, None, :], idx)
    mixed = jnp.dot(features, weight, preferred_element_type=F32)
    return mixed.astype(BF16)


def solution(mesh):
    placed = (
        P("seq", "head", None),
        P("seq", "head", None),
        P("seq", "head", None),
        P("seq", "head"),
        P("seq", "head"),
    )
    return jax.shard_map(
        on_device, mesh=mesh, in_specs=placed, out_specs=P("seq", "head"), check_vma=False
    )
```

time: 1140 us -> 123 us (0.11)
  waiting for transfers between devices: 613 us -> 9.91 us
  blocking collectives: 250 us -> 0 us
  other arithmetic: 223 us -> 0.02 us
  Pallas kernels: 0 us -> 88.4 us
  matrix products: 22.9 us -> 6.55 us
    all_gather x5 -> x1, waiting for transfers between devices: 612 us -> 9.2 us  [on_device(): weight = lax.all_gather(out_weight, 'seq', axis=0, tiled=True)]
    psum x1 -> x0, blocking collectives: 250 us -> none  [on_device(): all_totals, all_counts = lax.psum((totals, counts), 'seq')]
    add x126 -> x0, other arithmetic: 219 us -> none  [the longest x63 171 us: combine_parts(): out_first * factor_first[:, :, None]]
    pallas_call x0 -> x1, Pallas kernels: none -> 88.4 us  [chain(): pl.pallas_call(chain_kernel, out_shape=jax.ShapeDtypeStruct((TOK, 32 * E)...]
    dot_general x5 -> x1, matrix products: 22.9 us -> 6.55 us  [on_device(): mixed = jnp.dot(features, weight, preferred_element_type=F32)]
  transfers between devices with their start and end apart: 6 -> 1, of which waited for: 4 -> 1; matrix products, arithmetic and copies ran while one was open for 20% -> 3% of each run, Pallas kernels for 0% -> 72%
where the time goes in v1:
time: 123 us; the launch traced here: 122 us
  Pallas kernels  88.4 us (72%)
  between operations  13.4 us (11%)
  waiting for transfers between devices  9.91 us (8%)
  matrix products  6.55 us (5%)
  local copies, waits for them, and re-layouts  3.92 us (3%)
    pallas_call x1, Pallas kernels, chain(): pl.pallas_call(chain_kernel, out_shape=jax.ShapeDtypeStruct((TOK, 32 * E)...  88.4 us
    all_gather x1, waiting for transfers between devices, on_device(): weight = lax.all_gather(out_weight, 'seq', axis=0, tiled=True)  9.2 us
    dot_general x1, matrix products, on_device(): mixed = jnp.dot(features, weight, preferred_element_type=F32)  6.55 us
  transfers between devices with their start and end apart: 1, of which 1 were waited for; matrix products, arithmetic and copies ran while one was open for 3% of the time, Pallas kernels for 72%

profile of v1, /device:TPU:1, one launch (start us, length us, event | category | flops | bytes accessed | tf_op | source)
XLA Modules:
  0.0 122.3 jit_solution(2138716040069042001)
XLA Ops:
  6.5 0.0 all-gather.2.cloned.1.call-start
  6.5 0.7 all-gather.2.cloned.1.call-update
  7.3 0.7 reshape.3
  8.0 0.7 broadcast_in_dim.4.ids_ref
  8.7 1.1 copy.12
  9.8 1.4 %copy_bitcast_fusion = (bf16[8,256,128]{2,1,0:T(8,128)(2,1)S(1)}, bf16[8,256,128]{2,1,0:T(8,128)(2,1)S(1)}) fusion(bf16[256,8,128]{2,1,0:T(8,128)(2,1)} %param.7, bf16[256,8,128]{2,1,0:T(8,128)(2,1)} %param.6), kind=kLoop, calls=%fused_computation.1 | loop fusion | bytes 2097152 | tf_op jit(solution)/shard_map/transpose | solution.py:307
  11.2 88.4 %shard_map.55 = bf16[256,4096]{1,0:T(8,128)(2,1)S(1)} custom-call(bf16[8,256,128]{2,1,0:T(8,128)(2,1)S(1)} %bitcast.10, bf16[8,256,128]{2,1,0:T(8,128)(2,1)S(1)} %get-tuple-element.6.k_ref, bf16[8,256,128]{2,1,0:T(8,128)(2,1)S(1)} %get-tuple-element.5.v_ref, s32[8,1,256]{2,1,0:T(1,128)S(1)} %broadcast_in_dim.4.ids_ref, s32[2,8,256]{2,1,0:T(8,128)S(1)} %concatenate.7.idx_ref), custom_call_target="tpu_custom_call" | custom-call | flops 4000000000 | bytes 200000000 | tf_op jit(solution)/shard_map/pallas_call | solution.py:276
  99.7 9.2 %all-gather.2.cloned.1.call-done = bf16[4096,1024]{1,0:T(8,128)(2,1)} async-done(((bf16[64,1024]{1,0:T(8,128)(2,1)}), bf16[4096,1024]{1,0:T(8,128)(2,1)}) %all-gather.2.cloned.1.call-update) | async-done | bytes 8388624 | tf_op jit(solution)/shard_map/all_gather | solution.py:306
  108.9 6.6 %convolution_convert_fusion = bf16[256,1024]{1,0:T(8,128)(2,1)} fusion(bf16[256,4096]{1,0:T(8,128)(2,1)S(1)} %shard_map.55, bf16[4096,1024]{1,0:T(8,128)(2,1)} %all-gather.2.cloned.1.call-done), kind=kOutput, calls=%fused_computation | convolution fusion | flops 2147745792 | bytes 11010048 | tf_op jit(solution)/shard_map/dot_general | solution.py:309
  (2 shorter events, 0.0 us)
Async XLA Ops:
  6.5 102.3 %all-gather.2.cloned.1.call-start = ((), (), s32[]{:S(2)}) async-start(), calls=%async_computation | async-start | bytes 8519680 | tf_op jit(solution)/shard_map/all_gather | solution.py:306
Sparse Core Ops, SparseCore 0:
  10.1 98.7 all-gather.1

commit v2 on v1

--- a/solution.py
+++ b/solution.py
@@ -13,15 +13,16 @@
 TOK = 256
 BLK = C // NZ
 ROWS = BLK + 8
+HALF = E // 2
 EXP2_SCALE = math.log2(math.e) / math.sqrt(E)
 F32, BF16 = jnp.float32, jnp.bfloat16
 
 
 def chain_kernel(
-    q_ref, k_ref, v_ref, ids_ref, idx_ref, out_ref,
+    q_ref, k_ref, v_ref, ids_ref, idx_ref, w_ref, out_ref,
     qbuf, kbuf, vbuf, idbuf, idxbuf, acc, msg, recv_t, recv_o, cent, sbuf, mx, ls,
-    att, idcol, fsend, frecv,
-    ssem, rq, rk, rv, rid, ridx, rt, rc, ro, rz, ra, rb, rf, lsem,
+    att, idcol, wbuf, feat, psum, other,
+    ssem, rq, rk, rv, rid, ridx, rt, rc, ro, rz, ra, rb, rf, lsem, swc, rwo, rw1, rwr, rwl, rwy,
 ):
     s_id, x = lax.axis_index("seq"), lax.axis_index("head")
     c = lax.rem(s_id, 2)
@@ -44,6 +45,16 @@
         sends.append(cp)
         return cp
 
+    maybe = []
+
+    def put_if(cond, src, dst, rsem, seq, head):
+        cp = pltpu.make_async_remote_copy(
+            src_ref=src, dst_ref=dst, send_sem=swc.at[len(maybe)], recv_sem=rsem,
+            device_id=(seq, head), device_id_type=pl.DeviceIdType.MESH,
+        )
+        pl.when(cond)(cp.start)
+        maybe.append((cond, cp))
+
     def arrived(ref, rsem):
         pltpu.make_async_copy(ref, ref, rsem).wait()
 
@@ -60,6 +71,8 @@
         ty, tc = yc_peer(d)
         greet(seq_of(ty, z, tc), x)
         greet(seq_of(y, lax.rem(z + d, NZ), c), x)
+    for step in (1, NZ - 1):
+        greet(seq_of(y, lax.rem(z + step, NZ), 1 - c), x)
     for e in range(1, NX):
         greet(s_id, lax.rem(x + e, NX))
         greet(seq_of(y, z, 1 - c), lax.rem(x + e, NX))
@@ -75,7 +88,7 @@
         cp.start()
         local.append(cp)
 
-    pl.semaphore_wait(barrier, 20)
+    pl.semaphore_wait(barrier, 22)
 
     for src, buf, sem in ((ids_ref, idbuf, rid), (q_ref, qbuf, rq)):
         for d in range(1, 8):
@@ -92,6 +105,75 @@
             ty, tc = yc_peer(d)
             put(src.at[tc * NY + ty], buf.at[yc], sem.at[d - 1], seq_of(ty, z, tc), x)
 
+    home = lax.div(z, NZ // 2)
+    half_rows = pl.ds(pl.multiple_of(c * HALF, HALF), HALF)
+    other_rows = pl.ds(pl.multiple_of((1 - c) * HALF, HALF), HALF)
+
+    def w_slot(o):
+        return y * NY + lax.rem(o, NY)
+
+    def w_held(o):
+        return lax.div(o, NZ // 2) == c
+
+    w_own = wbuf.at[w_slot(z), half_rows]
+    w_copy = pltpu.make_async_copy(w_ref, w_own, lsem.at[5])
+    pl.when(home == c)(w_copy.start)
+    put_if(home != c, w_ref, w_own, rwo, seq_of(y, z, 1 - c), x)
+    for step, sem in ((1, 0), (NZ - 1, 2)):
+        put(w_ref, w_own, rw1.at[sem + c], seq_of(y, lax.rem(z + step, NZ), home), x)
+
+    def w_turn(k, far, sems, base):
+        o = lax.rem(z + far * k, NZ)
+        slot = w_slot(o)
+        if k == 1:
+            @pl.when(w_held(o))
+            def _():
+                for cc in range(2):
+                    arrived(wbuf.at[slot, pl.ds(cc * HALF, HALF)], rw1.at[base + cc])
+        else:
+            @pl.when(w_held(o))
+            def _():
+                arrived(wbuf.at[slot], sems.at[k - 2])
+        return o, slot
+
+    def w_step(k):
+        o, slot = w_turn(k, NZ - 1, rwr, 0)
+        put_if(w_held(o), wbuf.at[slot], wbuf.at[slot], rwr.at[k - 1], seq_of(y, lax.rem(z + 1, NZ), c), x)
+        if k < 3:
+            o, slot = w_turn(k, 1, rwl, 2)
+            put_if(w_held(o), wbuf.at[slot], wbuf.at[slot], rwl.at[k - 1],
+                   seq_of(y, lax.rem(z + NZ - 1, NZ), c), x)
+
+    def w_spread():
+        w_turn(4, NZ - 1, rwr, 0)
+        w_turn(3, 1, rwl, 2)
+
+        @pl.when(home == c)
+        def _():
+            w_copy.wait()
+            arrived(wbuf.at[w_slot(z), other_rows], rwo)
+
+        up, down = seq_of(lax.rem(y + 1, NY), z, c), seq_of(lax.rem(y + NY - 1, NY), z, c)
+        for n, (lo, to) in enumerate(((0, up), (2, down), (2, up), (0, down))):
+            rows = wbuf.at[pl.ds(y * NY + lo, 2)]
+            put(rows, rows, rwy.at[n], to, x)
+
+    def w_relay():
+        below, above = lax.rem(y + NY - 1, NY), lax.rem(y + 1, NY)
+        first = wbuf.at[pl.ds(below * NY, 2)]
+        arrived(first, rwy.at[0])
+        put(first, first, rwy.at[4], seq_of(above, z, c), x)
+        second = wbuf.at[pl.ds(above * NY + 2, 2)]
+        arrived(second, rwy.at[1])
+        put(second, second, rwy.at[5], seq_of(below, z, c), x)
+
+    def w_finish():
+        below, above, across = lax.rem(y + NY - 1, NY), lax.rem(y + 1, NY), lax.rem(y + 2, NY)
+        arrived(wbuf.at[pl.ds(below * NY + 2, 2)], rwy.at[2])
+        arrived(wbuf.at[pl.ds(above * NY, 2)], rwy.at[3])
+        arrived(wbuf.at[pl.ds(across * NY, 2)], rwy.at[4])
+        arrived(wbuf.at[pl.ds(across * NY + 2, 2)], rwy.at[5])
+
     def take8(buf, sem):
         for d in range(1, 8):
             arrived(buf.at[lax.rem(yc + 8 - d, 8)], sem.at[d - 1])
@@ -108,6 +190,7 @@
     local[1].wait()
     take8(idbuf, rid)
     take8(qbuf, rq)
+    w_step(1)
     acc[...] = jnp.zeros_like(acc)
 
     @pl.loop(0, 8)
@@ -130,6 +213,7 @@
             put(src.at[tz], recv.at[d - 1], sem.at[d - 1], seq_of(y, tz, c), x)
 
     reduce_z(recv_t, rt, msg.at[pl.ds(0, NZ)])
+    w_step(2)
 
     local[4].wait()
     for j in range(1, 8):
@@ -153,11 +237,13 @@
             put(buf.at[z], buf.at[z], sem.at[d - 1], seq_of(y, tz, c), x)
 
     gather_z(cent, rc)
+    w_step(3)
     local[2].wait()
     take8(kbuf, rk)
     for d in range(1, NZ):
         arrived(cent.at[lax.rem(z + NZ - d, NZ)], rc.at[d - 1])
 
+    w_spread()
     centroid = cent[...].reshape(C, E)
     mx[...] = jnp.full_like(mx, -jnp.inf)
 
@@ -209,6 +295,7 @@
     for d in range(1, NZ):
         tz = lax.rem(z + d, NZ)
         put(att.at[g0, z], att.at[g0, z], rz.at[d - 1], seq_of(y, tz, c), x)
+    w_relay()
     for d in range(1, NZ):
         arrived(att.at[g0, lax.rem(z + NZ - d, NZ)], rz.at[d - 1])
 
@@ -238,8 +325,6 @@
         to_y(g_of(e, 0), high, rb, e)
 
     lanes = lax.broadcasted_iota(jnp.int32, (2 * TOK, C), 1).astype(F32)
-    own = pl.ds(pl.multiple_of(c * TOK, TOK), TOK)
-    fcopies = []
     for dx in range(NX):
         xs = lax.rem(x + dx, NX)
         for dy in range(NY):
@@ -250,33 +335,43 @@
                 arrived(att.at[g, high], rb.at[dx * NY + dy])
             col = idcol[:, pl.ds(dx * 8 + dy, 1)]
             onehot = (lanes == col).astype(F32).astype(BF16)
-            feat = jnp.dot(onehot, att[g].reshape(C, E), preferred_element_type=F32).astype(BF16)
-            acc_rows = pl.ds(pl.multiple_of((xs * 8 + c * NY + lax.rem(y + dy, NY)) * E, E), E)
-            send_cols = pl.ds(pl.multiple_of(g * E, E), E)
-            mine = jnp.where(c == 0, feat[:TOK], feat[TOK:])
-            theirs = jnp.where(c == 0, feat[TOK:], feat[:TOK])
-            out_ref[:, acc_rows] = mine
-            fsend[:, send_cols] = theirs
-        cols = pl.ds(pl.multiple_of(xs * NY * E, NY * E), NY * E)
-        put(fsend.at[:, cols], frecv.at[:, cols], rf.at[dx], seq_of(y, z, 1 - c), x)
-    for dx in range(NX):
-        xs = lax.rem(x + dx, NX)
-        cols = pl.ds(pl.multiple_of(xs * NY * E, NY * E), NY * E)
-        arrived(frecv.at[:, cols], rf.at[dx])
-        there = pl.ds(pl.multiple_of(xs * 8 * E + (1 - c) * NY * E, NY * E), NY * E)
-        out_ref[:, there] = frecv[:, cols]
+            picked = jnp.dot(onehot, att[g].reshape(C, E), preferred_element_type=F32)
+            feat[:, pl.ds(pl.multiple_of(lax.rem(y + dy, NY) * E, E), E)] = picked.astype(BF16)
+        if dx == 0:
+            w_finish()
+        for order in range(2):
+            who = lax.rem(c + 1 + order, 2)
+            rows = pl.ds(pl.multiple_of(who * TOK, TOK), TOK)
+
+            @pl.loop(0, NX)
+            def _(n):
+                cols = pl.ds(pl.multiple_of(n * TOK, TOK), TOK)
+                block = wbuf[pl.ds(xs * NY, NY), :, cols].reshape(NY * E, TOK)
+                term = jnp.dot(feat[rows, :], block, preferred_element_type=F32)
+                if dx == 0:
+                    psum[rows, cols] = term
+                else:
+                    psum[rows, cols] += term
+
+            if dx == NX - 1 and order == 0:
+                put(psum.at[rows], other, rf.at[0], seq_of(y, z, 1 - c), x)
+    arrived(other, rf.at[0])
+    own = pl.ds(pl.multiple_of(c * TOK, TOK), TOK)
+    out_ref[...] = (psum[own, :] + other[...]).astype(BF16)
     for cp in sends:
         cp.wait_send()
-
-
-def chain(queries, keys, values, ids, idx):
+    for cond, cp in maybe:
+        pl.when(cond)(cp.wait_send)
+
+
+def chain(queries, keys, values, ids, idx, weight):
     vmem = pl.BlockSpec(memory_space=pltpu.VMEM)
     anyw = pl.BlockSpec(memory_space=pl.ANY)
     dma = pltpu.SemaphoreType.DMA
     return pl.pallas_call(
         chain_kernel,
-        out_shape=jax.ShapeDtypeStruct((TOK, 32 * E), BF16),
-        in_specs=[anyw, anyw, anyw, vmem, vmem],
+        out_shape=jax.ShapeDtypeStruct((TOK, 8 * E), BF16),
+        in_specs=[anyw, anyw, anyw, vmem, vmem, anyw],
         out_specs=vmem,
         scratch_shapes=[
             pltpu.VMEM((8, TOK, E), BF16), pltpu.VMEM((8, TOK, E), BF16), pltpu.VMEM((8, TOK, E), BF16),
@@ -286,15 +381,17 @@
             pltpu.VMEM((NZ, BLK, E), BF16), pltpu.VMEM((8, C, TOK), F32),
             pltpu.VMEM((C, E), F32), pltpu.VMEM((C, E), F32),
             pltpu.VMEM((16, NZ, BLK, E), BF16), pltpu.VMEM((2 * TOK, E), F32),
-            pltpu.VMEM((TOK, 16 * E), BF16), pltpu.VMEM((TOK, 16 * E), BF16),
-            dma((112,)), dma((7,)), dma((7,)), dma((7,)), dma((7,)), dma((8,)), dma((7,)), dma((7,)),
-            dma((7,)), dma((7,)), dma((16,)), dma((16,)), dma((4,)), dma((5,)),
+            pltpu.VMEM((16, E, 8 * E), BF16), pltpu.VMEM((2 * TOK, NY * E), BF16),
+            pltpu.VMEM((2 * TOK, 8 * E), F32), pltpu.VMEM((TOK, 8 * E), F32),
+            dma((120,)), dma((7,)), dma((7,)), dma((7,)), dma((7,)), dma((8,)), dma((7,)), dma((7,)),
+            dma((7,)), dma((7,)), dma((16,)), dma((16,)), dma((4,)), dma((6,)),
+            dma((8,)), dma(()), dma((4,)), dma((3,)), dma((2,)), dma((6,)),
         ],
         compiler_params=pltpu.CompilerParams(
             collective_id=0, has_side_effects=True, vmem_limit_bytes=48 * 1024 * 1024
         ),
         cost_estimate=pl.CostEstimate(flops=4_000_000_000, bytes_accessed=200_000_000, transcendentals=1 << 20),
-    )(queries, keys, values, ids, idx)
+    )(queries, keys, values, ids, idx, weight)
 
 
 def on_device(queries, keys, values, cluster_ids, out_weight):
@@ -303,11 +400,8 @@
     pair = ids.reshape(2, NY, TOK)
     pair = lax.dynamic_slice_in_dim(jnp.concatenate([pair, pair], axis=1), y, NY, axis=1)
     idx = jnp.concatenate([pair, jnp.zeros_like(pair)], axis=1)
-    weight = lax.all_gather(out_weight, "seq", axis=0, tiled=True)
     q, k, v = (jnp.transpose(a, (1, 0, 2)) for a in (queries, keys, values))
-    features = chain(q, k, v, ids[:, None, :], idx)
-    mixed = jnp.dot(features, weight, preferred_element_type=F32)
-    return mixed.astype(BF16)
+    return chain(q, k, v, ids[:, None, :], idx, out_weight)
 
 
 def solution(mesh):

time: 123 us -> 103 us (0.84)
  between operations: 13.4 us -> 0.06 us
  Pallas kernels: 88.4 us -> 99.2 us
  waiting for transfers between devices: 9.91 us -> 0 us
  matrix products: 6.55 us -> 0 us
    pallas_call x1, Pallas kernels: 88.4 us -> 99.2 us  [chain(): pl.pallas_call(chain_kernel, out_shape=jax.ShapeDtypeStruct((TOK, 8 * E),...]
    all_gather x1 -> x0, waiting for transfers between devices: 9.2 us -> none  [on_device(): weight = lax.all_gather(out_weight, 'seq', axis=0, tiled=True)]
    dot_general x1 -> x0, matrix products: 6.55 us -> none  [on_device(): mixed = jnp.dot(features, weight, preferred_element_type=F32)]
    unnamed x1 -> x10, local copies, waits for them, and re-layouts: 1.11 us -> 3.54 us
  transfers between devices with their start and end apart: 1 -> 0, of which waited for: 1 -> 0; matrix products, arithmetic and copies ran while one was open for 3% -> 0% of each run, Pallas kernels for 72% -> 0%
where the time goes in v2:
time: 103 us
  Pallas kernels  99.2 us (96%)
  local copies, waits for them, and re-layouts  3.74 us (4%)
    pallas_call x1, Pallas kernels, chain(): pl.pallas_call(chain_kernel, out_shape=jax.ShapeDtypeStruct((TOK, 8 * E),...  99.2 us
    unnamed x10, local copies, waits for them, and re-layouts  3.54 us

profile of v2, /device:TPU:1, one launch (start us, length us, event | category | flops | bytes accessed | tf_op | source)
XLA Modules:
  0.0 103.1 jit_solution(7839739081113476305)
XLA Ops:
  0.0 0.0 copy-start.3
  0.0 0.7 copy-done.3
  0.8 0.0 copy-start.1
  0.8 0.0 copy-start.2
  0.8 1.2 %copy.12 = bf16[256,8,128]{2,0,1:T(8,128)(2,1)S(1)} copy(bf16[256,8,128]{2,1,0:T(8,128)(2,1)} %param.5) | data formatting | bytes 1048576 | tf_op args[0]
  2.0 0.0 copy-done.1
  2.0 0.1 copy-done.2
  2.1 0.0 copy-start
  2.1 0.2 copy_bitcast_fusion
  2.3 0.7 copy-done
  3.0 99.2 %shard_map.55 = bf16[256,1024]{1,0:T(8,128)(2,1)S(1)} custom-call(bf16[8,256,128]{2,1,0:T(8,128)(2,1)S(1)} %bitcast.8, bf16[8,256,128]{2,1,0:T(8,128)(2,1)S(1)} %get-tuple-element.6.k_ref, bf16[8,256,128]{2,1,0:T(8,128)(2,1)S(1)} %get-tuple-element.5.v_ref, s32[8,1,256]{2,1,0:T(1,128)S(1)} %broadcast_in_dim.4.ids_ref, s32[2,8,256]{2,1,0:T(8,128)S(1)} %concatenate.7.idx_ref, ...), custom_call_target="tpu_custom_call" | custom-call | flops 4000000000 | bytes 200000000 | tf_op jit(solution)/shard_map/pallas_call | solution.py:371
  102.3 0.8 copy.14
  (4 shorter events, 0.0 us)
Async XLA Ops:
  0.0 0.7 copy-start.3
  0.8 1.2 %copy-start.1 = (bf16[256,8,128]{2,1,0:T(8,128)(2,1)S(1)}, bf16[256,8,128]{2,1,0:T(8,128)(2,1)}, u32[]{:S(2)}) copy-start(bf16[256,8,128]{2,1,0:T(8,128)(2,1)} %param.7) | copy-start | bytes 1572868
  0.8 1.4 %copy-start.2 = (bf16[256,8,128]{2,1,0:T(8,128)(2,1)S(1)}, bf16[256,8,128]{2,1,0:T(8,128)(2,1)}, u32[]{:S(2)}) copy-start(bf16[256,8,128]{2,1,0:T(8,128)(2,1)} %param.6) | copy-start | bytes 1572868
  2.1 0.9 copy-start

commit v3 on v2

v3 whole, which is shorter than its diff:
```python
import math

import jax
import jax.numpy as jnp
from jax import lax
from jax.experimental import pallas as pl
from jax.experimental.pallas import tpu as pltpu
from jax.sharding import PartitionSpec as P

C = 512
E = 128
NY, NZ, NX = 4, 8, 4
TOK = 256
BLK = C // NZ
HALF = E // 2
EXP2_SCALE = math.log2(math.e) / math.sqrt(E)
F32, BF16 = jnp.float32, jnp.bfloat16
SIDE = 384
SUM_T, OUT_T = BF16, BF16


def chain_kernel(
    q_ref, k_ref, v_ref, ids_ref, idx_ref, w_ref, out_ref,
    qbuf, kbuf, vbuf, idbuf, idxbuf, acc, msg_t, msg_c, msg_o, msg_m, recv_t, recv_c, recv_o, recv_m, cent, sbuf, mx, ls, oacc,
    att, idcol, wbuf, feat, psum, other,
    ssem, rq, rk, rv, rid, ridx, rt, rtc, rc, ro, rom, rz, ra, rb, rf, lsem, swc, rwo, rw1, rwr, rwl, rwy, rwa, rwra, rwla,
):
    s_id, x = lax.axis_index("seq"), lax.axis_index("head")
    c = lax.rem(s_id, 2)
    z = lax.rem(lax.div(s_id, 2), NZ)
    y = lax.div(s_id, 2 * NZ)
    yc = y * 2 + c
    g0 = x * NY + y

    def seq_of(yy, zz, cc):
        return (yy * NZ + zz) * 2 + cc

    sends = []

    def put(src, dst, rsem, seq, head):
        cp = pltpu.make_async_remote_copy(
            src_ref=src, dst_ref=dst, send_sem=ssem.at[len(sends)], recv_sem=rsem,
            device_id=(seq, head), device_id_type=pl.DeviceIdType.MESH,
        )
        cp.start()
        sends.append(cp)
        return cp

    maybe = []

    def put_if(cond, src, dst, rsem, seq, head):
        cp = pltpu.make_async_remote_copy(
            src_ref=src, dst_ref=dst, send_sem=swc.at[len(maybe)], recv_sem=rsem,
            device_id=(seq, head), device_id_type=pl.DeviceIdType.MESH,
        )
        pl.when(cond)(cp.start)
        maybe.append((cond, cp))

    def arrived(ref, rsem):
        pltpu.make_async_copy(ref, ref, rsem).wait()

    def yc_peer(d):
        t = lax.rem(yc + d, 8)
        return lax.div(t, 2), lax.rem(t, 2)

    barrier = pltpu.get_barrier_semaphore()

    def greet(seq, head):
        pl.semaphore_signal(barrier, inc=1, device_id=(seq, head), device_id_type=pl.DeviceIdType.MESH)

    for d in range(1, 8):
        ty, tc = yc_peer(d)
        greet(seq_of(ty, z, tc), x)
        greet(seq_of(y, lax.rem(z + d, NZ), c), x)
    for step in (1, NZ - 1):
        greet(seq_of(y, lax.rem(z + step, NZ), 1 - c), x)
    for e in range(1, NX):
        greet(s_id, lax.rem(x + e, NX))
        greet(seq_of(y, z, 1 - c), lax.rem(x + e, NX))

    local = []
    own_h = c * NY + y
    for n, (src, dst) in enumerate(
        ((ids_ref.at[own_h], idbuf.at[yc]), (q_ref.at[own_h], qbuf.at[yc]),
         (k_ref.at[own_h], kbuf.at[yc]), (v_ref.at[own_h], vbuf.at[yc]),
         (idx_ref.at[c], idxbuf.at[c]))
    ):
        cp = pltpu.make_async_copy(src, dst, lsem.at[n])
        cp.start()
        local.append(cp)

    pl.semaphore_wait(barrier, 22)

    for src, buf, sem in ((ids_ref, idbuf, rid), (q_ref, qbuf, rq)):
        for d in range(1, 8):
            ty, tc = yc_peer(d)
            put(src.at[tc * NY + ty], buf.at[yc], sem.at[d - 1], seq_of(ty, z, tc), x)
    put(idx_ref.at[1 - c], idxbuf.at[c], ridx.at[1], seq_of(y, z, 1 - c), x)
    for e in range(1, NX):
        for f in range(2):
            tc = lax.rem(c + f, 2)
            put(idx_ref.at[tc], idxbuf.at[(NX - e) * 2 + c], ridx.at[(NX - e) * 2 + f],
                seq_of(y, z, tc), lax.rem(x + e, NX))
    for src, buf, sem in ((k_ref, kbuf, rk), (v_ref, vbuf, rv)):
        for d in range(1, 8):
            ty, tc = yc_peer(d)
            put(src.at[tc * NY + ty], buf.at[yc], sem.at[d - 1], seq_of(ty, z, tc), x)

    home = lax.div(z, NZ // 2)
    half_rows = pl.ds(pl.multiple_of(c * HALF, HALF), HALF)
    other_rows = pl.ds(pl.multiple_of((1 - c) * HALF, HALF), HALF)

    def w_held(o):
        return lax.div(o, NZ // 2) == c

    left_cols, right_cols = pl.ds(0, SIDE), pl.ds(SIDE, 8 * E - SIDE)

    def w_b(o):
        return wbuf.at[y, lax.rem(o, NY), :, right_cols]

    def w_a(o):
        return wbuf.at[:, lax.rem(o, NY), :, left_cols]

    w_own = wbuf.at[y, lax.rem(z, NY), half_rows]
    w_copy = pltpu.make_async_copy(w_ref, w_own, lsem.at[5])
    pl.when(home == c)(w_copy.start)
    put_if(home != c, w_ref, w_own, rwo, seq_of(y, z, 1 - c), x)
    own_b = wbuf.at[y, lax.rem(z, NY), half_rows, right_cols]
    for step, sem in ((1, 0), (NZ - 1, 2)):
        put(w_ref.at[:, right_cols], own_b, rw1.at[sem + c], seq_of(y, lax.rem(z + step, NZ), home), x)

    def w_side():
        own_a = wbuf.at[y, lax.rem(z, NY), half_rows, left_cols]
        for e in range(1, NY):
            put(w_ref.at[:, left_cols], own_a, rwa.at[(e - 1) * 2 + c], seq_of(lax.rem(y + e, NY), z, home), x)

    w_side()

    def w_turn(k, far, sems, base):
        o = lax.rem(z + far * k, NZ)

        @pl.when(w_held(o))
        def _():
            if k == 1:
                for cc in range(2):
                    arrived(wbuf.at[y, lax.rem(o, NY), pl.ds(cc * HALF, HALF), right_cols], rw1.at[base + cc])
            else:
                arrived(w_b(o), sems.at[k - 2])

        return o

    def w_step(k):
        o = w_turn(k, NZ - 1, rwr, 0)
        put_if(w_held(o), w_b(o), w_b(o), rwr.at[k - 1], seq_of(y, lax.rem(z + 1, NZ), c), x)
        if k < 3:
            o = w_turn(k, 1, rwl, 2)
            put_if(w_held(o), w_b(o), w_b(o), rwl.at[k - 1], seq_of(y, lax.rem(z + NZ - 1, NZ), c), x)

    def w_spread():
        w_turn(4, NZ - 1, rwr, 0)
        w_turn(3, 1, rwl, 2)

        @pl.when(home == c)
        def _():
            w_copy.wait()
            arrived(wbuf.at[y, lax.rem(z, NY), other_rows], rwo)

        up, down = seq_of(lax.rem(y + 1, NY), z, c), seq_of(lax.rem(y + NY - 1, NY), z, c)
        for n, (lo, to) in enumerate(((0, up), (2, down), (2, up), (0, down))):
            rows = wbuf.at[y, pl.ds(lo, 2), :, right_cols]
            put(rows, rows, rwy.at[n], to, x)

    def w_relay():
        below, above = lax.rem(y + NY - 1, NY), lax.rem(y + 1, NY)
        first = wbuf.at[below, pl.ds(0, 2), :, right_cols]
        arrived(first, rwy.at[0])
        put(first, first, rwy.at[4], seq_of(above, z, c), x)
        second = wbuf.at[above, pl.ds(2, 2), :, right_cols]
        arrived(second, rwy.at[1])
        put(second, second, rwy.at[5], seq_of(below, z, c), x)

    def w_finish():
        below, above, across = lax.rem(y + NY - 1, NY), lax.rem(y + 1, NY), lax.rem(y + 2, NY)
        arrived(wbuf.at[below, pl.ds(2, 2), :, right_cols], rwy.at[2])
        arrived(wbuf.at[above, pl.ds(0, 2), :, right_cols], rwy.at[3])
        arrived(wbuf.at[across, pl.ds(0, 2), :, right_cols], rwy.at[4])
        arrived(wbuf.at[across, pl.ds(2, 2), :, right_cols], rwy.at[5])
        a_wait(4, NZ - 1, rwra)
        a_wait(3, 1, rwla)

    def a_wait(k, far, sems):
        o = lax.rem(z + far * k, NZ)

        @pl.when(w_held(o))
        def _():
            arrived(w_a(o), sems.at[k - 1])

    def a_step(k):
        if k == 0:
            @pl.when(home == c)
            def _():
                for e in range(1, NY):
                    for cc in range(2):
                        arrived(wbuf.at[lax.rem(y + NY - e, NY), lax.rem(z, NY), pl.ds(cc * HALF, HALF), left_cols],
                                rwa.at[(e - 1) * 2 + cc])
        else:
            a_wait(k, NZ - 1, rwra)
            if k < 3:
                a_wait(k, 1, rwla)
        o = lax.rem(z + (NZ - 1) * k, NZ)
        put_if(w_held(o), w_a(o), w_a(o), rwra.at[k], seq_of(y, lax.rem(z + 1, NZ), c), x)
        if k < 3:
            o = lax.rem(z + k, NZ)
            put_if(w_held(o), w_a(o), w_a(o), rwla.at[k], seq_of(y, lax.rem(z + NZ - 1, NZ), c), x)

    def take8(buf, sem):
        for d in range(1, 8):
            arrived(buf.at[lax.rem(yc + 8 - d, 8)], sem.at[d - 1])

    eye = lax.broadcasted_iota(jnp.int32, (BLK, E), 0) == lax.broadcasted_iota(jnp.int32, (BLK, E), 1)

    def to_row(col):
        return jnp.sum(jnp.where(eye, col, 0.0), axis=0, keepdims=True)

    def to_col(row):
        return jnp.sum(jnp.where(eye, row, 0.0), axis=1, keepdims=True)

    local[0].wait()
    local[1].wait()
    acc[...] = jnp.zeros_like(acc)

    @pl.loop(0, 8)
    def _(d):
        i = lax.rem(yc + 8 - d, 8)

        @pl.when(d > 0)
        def _():
            arrived(idbuf.at[i], rid.at[d - 1])
            arrived(qbuf.at[i], rq.at[d - 1])

        label = lax.broadcasted_iota(jnp.int32, (C, TOK), 0)
        onehot = (label == idbuf[i]).astype(F32).astype(BF16)
        rhs = jnp.concatenate([qbuf[i], jnp.ones((TOK, E), BF16)], axis=1)
        acc[...] += jnp.dot(onehot, rhs, preferred_element_type=F32)

    @pl.loop(0, NZ)
    def _(b):
        rows = pl.ds(pl.multiple_of(b * BLK, BLK), BLK)
        msg_t[b] = acc[rows, pl.ds(0, E)].astype(SUM_T)
        msg_c[b] = jnp.broadcast_to(to_row(acc[rows, pl.ds(E, E)]), (8, E))

    for d in (4, 3, 5, 2, 6, 1, 7):
        tz = lax.rem(z + d, NZ)
        put(msg_c.at[tz], recv_c.at[d - 1], rtc.at[d - 1], seq_of(y, tz, c), x)
        put(msg_t.at[tz], recv_t.at[d - 1], rt.at[d - 1], seq_of(y, tz, c), x)
    w_step(1)

    local[4].wait()
    for j in range(1, 8):
        e, f = j // 2, j % 2
        arrived(idxbuf.at[e * 2 + lax.rem(c + f, 2)], ridx.at[j])
    for half in range(2):
        rows = jnp.concatenate([idxbuf[e * 2 + half] for e in range(NX)], axis=0).astype(F32)
        rows = jnp.concatenate([rows, jnp.zeros((E - 8 * NX, TOK), F32)], axis=0)
        idcol[pl.ds(half * TOK, TOK), :] = rows.T

    w_step(2)
    total, count = msg_t[z].astype(F32), msg_c[z]
    for d in range(1, NZ):
        arrived(recv_c.at[d - 1], rtc.at[d - 1])
        arrived(recv_t.at[d - 1], rt.at[d - 1])
        total = total + recv_t[d - 1].astype(F32)
        count = count + recv_c[d - 1]
    count = to_col(count[:1])
    cent[z] = (total / jnp.maximum(count, 1.0)).astype(BF16)

    for d in (4, 3, 5, 2, 6, 1, 7):
        tz = lax.rem(z + d, NZ)
        put(cent.at[z], cent.at[z], rc.at[d - 1], seq_of(y, tz, c), x)
    w_step(3)
    local[2].wait()
    take8(kbuf, rk)
    for d in range(1, NZ):
        arrived(cent.at[lax.rem(z + NZ - d, NZ)], rc.at[d - 1])

    w_spread()
    a_step(0)
    half = C // 2
    for part, dist in enumerate(((4, 3, 5, 2), (6, 1, 7, 0))):
        centroid = jnp.concatenate([cent[lax.rem(z + d, NZ)] for d in dist], axis=0)
        mx[...] = jnp.full_like(mx, -jnp.inf)

        @pl.loop(0, 8)
        def _(i):
            s = lax.dot_general(centroid, kbuf[i], (((1,), (1,)), ((), ())), preferred_element_type=F32)
            sbuf[i] = s
            mx[...] = jnp.maximum(mx[...], jnp.maximum(s[:, :E], s[:, E:]))

        mx[...] = jnp.broadcast_to(jnp.max(mx[...], axis=1, keepdims=True), (half, E))
        ls[...] = jnp.zeros_like(ls)
        if part == 0:
            local[3].wait()
            take8(vbuf, rv)
        oacc[...] = jnp.zeros_like(oacc)

        @pl.loop(0, 8)
        def _(i):
            m = mx[...]
            p = jnp.exp2((sbuf[i] - jnp.concatenate([m, m], axis=1)) * EXP2_SCALE)
            ls[...] += p[:, :E] + p[:, E:]
            oacc[...] += jnp.dot(p.astype(BF16), vbuf[i], preferred_element_type=F32)

        ls[...] = jnp.broadcast_to(jnp.sum(ls[...], axis=1, keepdims=True), (half, E))
        first = lax.broadcasted_iota(jnp.int32, (8, E), 0) == 0
        for j, d in enumerate(dist):
            rows = pl.ds(j * BLK, BLK)
            msg_m[d] = jnp.where(first, to_row(mx[rows, :]), to_row(ls[rows, :]))
            msg_o[d] = oacc[rows, :].astype(OUT_T)
            if d > 0:
                tz = lax.rem(z + d, NZ)
                put(msg_m.at[d], recv_m.at[d - 1], rom.at[d - 1], seq_of(y, tz, c), x)
                put(msg_o.at[d], recv_o.at[d - 1], ro.at[d - 1], seq_of(y, tz, c), x)

    a_step(1)
    stats, parts = [msg_m[0]], [msg_o[0]]
    for d in range(1, NZ):
        arrived(recv_m.at[d - 1], rom.at[d - 1])
        arrived(recv_o.at[d - 1], ro.at[d - 1])
        stats.append(recv_m[d - 1])
        parts.append(recv_o[d - 1])
    tops = [to_col(stat[:1]) for stat in stats]
    largest = tops[0]
    for t in tops[1:]:
        largest = jnp.maximum(largest, t)
    num, den = 0.0, 0.0
    for stat, part, t in zip(stats, parts, tops):
        factor = jnp.exp2((t - largest) * EXP2_SCALE)
        num = num + part.astype(F32) * factor
        den = den + to_col(stat[1:2]) * factor
    att[g0, z] = (num / den).astype(BF16)

    for d in (4, 3, 5, 2, 6, 1, 7):
        tz = lax.rem(z + d, NZ)
        put(att.at[g0, z], att.at[g0, z], rz.at[d - 1], seq_of(y, tz, c), x)
    w_relay()
    a_step(2)
    for d in range(1, NZ):
        arrived(att.at[g0, lax.rem(z + NZ - d, NZ)], rz.at[d - 1])

    a_step(3)
    low, high = pl.ds(0, NZ // 2), pl.ds(NZ // 2, NZ // 2)

    def g_of(dx, dy):
        return lax.rem(x + dx, NX) * NY + lax.rem(y + dy, NY)

    def to_y(g, part, sem, dx):
        for e in range(1, NY):
            put(att.at[g, part], att.at[g, part], sem.at[dx * NY + NY - e],
                seq_of(lax.rem(y + e, NY), z, c), x)

    def to_x(g, part, sem, dy):
        for e in range(1, NX):
            put(att.at[g, part], att.at[g, part], sem.at[(NX - e) * NY + dy],
                s_id, lax.rem(x + e, NX))

    to_y(g0, low, ra, 0)
    to_x(g0, high, rb, 0)
    to_x(g0, low, ra, 0)
    to_y(g0, high, rb, 0)
    for e in range(1, NY):
        arrived(att.at[g_of(0, e), low], ra.at[e])
        to_x(g_of(0, e), low, ra, e)
        arrived(att.at[g_of(e, 0), high], rb.at[e * NY])
        to_y(g_of(e, 0), high, rb, e)

    lanes = lax.broadcasted_iota(jnp.int32, (2 * TOK, C), 1).astype(F32)
    groups = (
        ((0, 0), (0, 1), (0, 2), (0, 3)),
        ((1, 0), (2, 0), (3, 0)),
        ((1, 1), (1, 2), (2, 1), (2, 2)),
        ((1, 3), (3, 1), (2, 3), (3, 2), (3, 3)),
    )
    mine = pl.ds(pl.multiple_of(c * TOK, TOK), TOK)
    theirs = pl.ds(pl.multiple_of((1 - c) * TOK, TOK), TOK)
    for at, heads in enumerate(groups):
        for n, (dx, dy) in enumerate(heads):
            g = g_of(dx, dy)
            if dx > 0:
                arrived(att.at[g, low], ra.at[dx * NY + dy])
            if dy > 0:
                arrived(att.at[g, high], rb.at[dx * NY + dy])
            col = idcol[:, pl.ds(dx * 8 + dy, 1)]
            onehot = (lanes == col).astype(F32).astype(BF16)
            picked = jnp.dot(onehot, att[g].reshape(C, E), preferred_element_type=F32)
            feat[:, pl.ds(n * E, E)] = picked.astype(BF16)
        if at == 0:
            w_finish()

        def term(rows, cols):
            block = jnp.concatenate(
                [wbuf[lax.rem(x + dx, NX), lax.rem(y + dy, NY), :, cols] for dx, dy in heads], axis=0
            )
            return jnp.dot(feat[rows, pl.ds(0, len(heads) * E)], block, preferred_element_type=F32)

        if at < len(groups) - 1:
            @pl.loop(0, NX)
            def _(n):
                cols = pl.ds(pl.multiple_of(n * TOK, TOK), TOK)
                if at == 0:
                    psum[:, cols] = term(slice(None), cols)
                else:
                    psum[:, cols] += term(slice(None), cols)
        else:
            for n in range(NX):
                cols = pl.ds(n * TOK, TOK)
                psum[theirs, cols] += term(theirs, cols)
                put(psum.at[theirs, cols], other.at[:, cols], rf.at[n], seq_of(y, z, 1 - c), x)
            for n in range(NX):
                cols = pl.ds(n * TOK, TOK)
                total = psum[mine, cols] + term(mine, cols)
                arrived(other.at[:, cols], rf.at[n])
                out_ref[:, cols] = (total + other[:, cols]).astype(BF16)
    for cp in sends:
        cp.wait_send()
    for cond, cp in maybe:
        pl.when(cond)(cp.wait_send)


def chain(queries, keys, values, ids, idx, weight):
    vmem = pl.BlockSpec(memory_space=pltpu.VMEM)
    anyw = pl.BlockSpec(memory_space=pl.ANY)
    dma = pltpu.SemaphoreType.DMA
    return pl.pallas_call(
        chain_kernel,
        out_shape=jax.ShapeDtypeStruct((TOK, 8 * E), BF16),
        in_specs=[anyw, anyw, anyw, vmem, vmem, anyw],
        out_specs=vmem,
        scratch_shapes=[
            pltpu.VMEM((8, TOK, E), BF16), pltpu.VMEM((8, TOK, E), BF16), pltpu.VMEM((8, TOK, E), BF16),
            pltpu.VMEM((8, 1, TOK), jnp.int32), pltpu.VMEM((8, 8, TOK), jnp.int32),
            pltpu.VMEM((C, 2 * E), F32),
            pltpu.VMEM((NZ, BLK, E), SUM_T), pltpu.VMEM((NZ, 8, E), F32),
            pltpu.VMEM((NZ, BLK, E), OUT_T), pltpu.VMEM((NZ, 8, E), F32),
            pltpu.VMEM((NZ - 1, BLK, E), SUM_T), pltpu.VMEM((NZ - 1, 8, E), F32),
            pltpu.VMEM((NZ - 1, BLK, E), OUT_T), pltpu.VMEM((NZ - 1, 8, E), F32),
            pltpu.VMEM((NZ, BLK, E), BF16), pltpu.VMEM((8, C // 2, TOK), F32),
            pltpu.VMEM((C // 2, E), F32), pltpu.VMEM((C // 2, E), F32), pltpu.VMEM((C // 2, E), F32),
            pltpu.VMEM((16, NZ, BLK, E), BF16), pltpu.VMEM((2 * TOK, E), F32),
            pltpu.VMEM((NX, NY, E, 8 * E), BF16), pltpu.VMEM((2 * TOK, 5 * E), BF16),
            pltpu.VMEM((2 * TOK, 8 * E), F32), pltpu.VMEM((TOK, 8 * E), F32),
            dma((144,)), dma((7,)), dma((7,)), dma((7,)), dma((7,)), dma((8,)),
            dma((7,)), dma((7,)), dma((7,)), dma((7,)), dma((7,)), dma((7,)),
            dma((16,)), dma((16,)), dma((4,)), dma((6,)),
            dma((16,)), dma(()), dma((4,)), dma((3,)), dma((2,)), dma((6,)), dma((6,)), dma((4,)), dma((3,)),
        ],
        compiler_params=pltpu.CompilerParams(
            collective_id=0, has_side_effects=True, vmem_limit_bytes=48 * 1024 * 1024
        ),
        cost_estimate=pl.CostEstimate(flops=4_000_000_000, bytes_accessed=200_000_000, transcendentals=1 << 20),
    )(queries, keys, values, ids, idx, weight)


def on_device(queries, keys, values, cluster_ids, out_weight):
    y = lax.div(lax.axis_index("seq"), 2 * NZ)
    ids = cluster_ids.T
    pair = ids.reshape(2, NY, TOK)
    pair = lax.dynamic_slice_in_dim(jnp.concatenate([pair, pair], axis=1), y, NY, axis=1)
    idx = jnp.concatenate([pair, jnp.zeros_like(pair)], axis=1)
    q, k, v = (jnp.transpose(a, (1, 0, 2)) for a in (queries, keys, values))
    return chain(q, k, v, ids[:, None, :], idx, out_weight)


def solution(mesh):
    placed = (
        P("seq", "head", None),
        P("seq", "head", None),
        P("seq", "head", None),
        P("seq", "head"),
        P("seq", "head"),
    )
    return jax.shard_map(
        on_device, mesh=mesh, in_specs=placed, out_specs=P("seq", "head"), check_vma=False
    )
```

time: 103 us -> 84.4 us (0.82)
  Pallas kernels: 99.2 us -> 80.4 us
    pallas_call x1, Pallas kernels: 99.2 us -> 80.4 us  [chain(): pl.pallas_call(chain_kernel, out_shape=jax.ShapeDtypeStruct((TOK, 8 * E),...]
where the time goes in v3:
time: 84.4 us; the launch traced here: 84.2 us
  Pallas kernels  80.4 us (95%)
  local copies, waits for them, and re-layouts  3.74 us (4%)
    pallas_call x1, Pallas kernels, chain(): pl.pallas_call(chain_kernel, out_shape=jax.ShapeDtypeStruct((TOK, 8 * E),...  80.4 us
    unnamed x10, local copies, waits for them, and re-layouts  3.54 us

profile of v3, /device:TPU:1, one launch (start us, length us, event | category | flops | bytes accessed | tf_op | source)
XLA Modules:
  0.0 84.2 jit_solution(11471133602697843088)
XLA Ops:
  0.0 0.0 copy-start.3
  0.0 0.7 copy-done.3
  0.8 0.0 copy-start.1
  0.8 0.0 copy-start.2
  0.8 1.2 %copy.12 = bf16[256,8,128]{2,0,1:T(8,128)(2,1)S(1)} copy(bf16[256,8,128]{2,1,0:T(8,128)(2,1)} %param.5) | data formatting | bytes 1048576 | tf_op args[0]
  2.0 0.0 copy-done.1
  2.0 0.1 copy-done.2
  2.1 0.0 copy-start
  2.1 0.2 copy_bitcast_fusion
  2.3 0.7 copy-done
  3.0 80.4 %shard_map.55 = bf16[256,1024]{1,0:T(8,128)(2,1)S(1)} custom-call(bf16[8,256,128]{2,1,0:T(8,128)(2,1)S(1)} %bitcast.8, bf16[8,256,128]{2,1,0:T(8,128)(2,1)S(1)} %get-tuple-element.6.k_ref, bf16[8,256,128]{2,1,0:T(8,128)(2,1)S(1)} %get-tuple-element.5.v_ref, s32[8,1,256]{2,1,0:T(1,128)S(1)} %broadcast_in_dim.4.ids_ref, s32[2,8,256]{2,1,0:T(8,128)S(1)} %concatenate.7.idx_ref, ...), custom_call_target="tpu_custom_call" | custom-call | flops 4000000000 | bytes 200000000 | tf_op jit(solution)/shard_map/pallas_call | solution.py:433
  83.4 0.8 copy.14
  (4 shorter events, 0.0 us)
Async XLA Ops:
  0.0 0.7 copy-start.3
  0.8 1.2 %copy-start.1 = (bf16[256,8,128]{2,1,0:T(8,128)(2,1)S(1)}, bf16[256,8,128]{2,1,0:T(8,128)(2,1)}, u32[]{:S(2)}) copy-start(bf16[256,8,128]{2,1,0:T(8,128)(2,1)} %param.7) | copy-start | bytes 1572868
  0.8 1.4 %copy-start.2 = (bf16[256,8,128]{2,1,0:T(8,128)(2,1)S(1)}, bf16[256,8,128]{2,1,0:T(8,128)(2,1)}, u32[]{:S(2)}) copy-start(bf16[256,8,128]{2,1,0:T(8,128)(2,1)} %param.6) | copy-start | bytes 1572868
  2.1 0.9 %copy-start = (bf16[64,1024]{1,0:T(8,128)(2,1)S(1)}, bf16[64,1024]{1,0:T(8,128)(2,1)}, u32[]{:S(2)}) copy-start(bf16[64,1024]{1,0:T(8,128)(2,1)} %w_ref.1) | copy-start | bytes 393220

commit v4 on v3

--- a/solution.py
+++ b/solution.py
@@ -15,15 +15,15 @@
 HALF = E // 2
 EXP2_SCALE = math.log2(math.e) / math.sqrt(E)
 F32, BF16 = jnp.float32, jnp.bfloat16
-SIDE = 384
+SIDE = 256
 SUM_T, OUT_T = BF16, BF16
 
 
 def chain_kernel(
-    q_ref, k_ref, v_ref, ids_ref, idx_ref, w_ref, out_ref,
-    qbuf, kbuf, vbuf, idbuf, idxbuf, acc, msg_t, msg_c, msg_o, msg_m, recv_t, recv_c, recv_o, recv_m, cent, sbuf, mx, ls, oacc,
-    att, idcol, wbuf, feat, psum, other,
-    ssem, rq, rk, rv, rid, ridx, rt, rtc, rc, ro, rom, rz, ra, rb, rf, lsem, swc, rwo, rw1, rwr, rwl, rwy, rwa, rwra, rwla,
+    q_ref, k_ref, v_ref, ids_ref, w_ref, out_ref,
+    qbuf, kbuf, vbuf, idst, idbuf, idxbuf, acc, msg_t, msg_c, msg_o, msg_m, recv_t, recv_c, recv_o, recv_m, cent, sbuf, mx, ls, oacc,
+    att, idrow, idcol, wbuf, feat, psum, other,
+    ssem, rq, rk, rv, rid, ridx, rt, rtc, rc, ro, rom, rz, ra, rb, rf, lsem, swc, rwo, rw1, rwr, rwl, rwy, rwa, rwra, rwla, zup, zdown,
 ):
     s_id, x = lax.axis_index("seq"), lax.axis_index("head")
     c = lax.rem(s_id, 2)
@@ -71,35 +71,39 @@
     for d in range(1, 8):
         ty, tc = yc_peer(d)
         greet(seq_of(ty, z, tc), x)
-        greet(seq_of(y, lax.rem(z + d, NZ), c), x)
     for step in (1, NZ - 1):
-        greet(seq_of(y, lax.rem(z + step, NZ), 1 - c), x)
+        greet(seq_of(y, lax.rem(z + step, NZ), 0), x)
+        greet(seq_of(y, lax.rem(z + step, NZ), 1), x)
     for e in range(1, NX):
         greet(s_id, lax.rem(x + e, NX))
         greet(seq_of(y, z, 1 - c), lax.rem(x + e, NX))
 
+    for h in range(8):
+        idst[h] = ids_ref[pl.ds(h, 1), :]
     local = []
     own_h = c * NY + y
     for n, (src, dst) in enumerate(
-        ((ids_ref.at[own_h], idbuf.at[yc]), (q_ref.at[own_h], qbuf.at[yc]),
+        ((idst.at[own_h], idbuf.at[yc]), (q_ref.at[own_h], qbuf.at[yc]),
          (k_ref.at[own_h], kbuf.at[yc]), (v_ref.at[own_h], vbuf.at[yc]),
-         (idx_ref.at[c], idxbuf.at[c]))
+         (ids_ref, idxbuf.at[c]))
     ):
         cp = pltpu.make_async_copy(src, dst, lsem.at[n])
         cp.start()
         local.append(cp)
 
-    pl.semaphore_wait(barrier, 22)
-
-    for src, buf, sem in ((ids_ref, idbuf, rid), (q_ref, qbuf, rq)):
-        for d in range(1, 8):
-            ty, tc = yc_peer(d)
-            put(src.at[tc * NY + ty], buf.at[yc], sem.at[d - 1], seq_of(ty, z, tc), x)
-    put(idx_ref.at[1 - c], idxbuf.at[c], ridx.at[1], seq_of(y, z, 1 - c), x)
+    pl.semaphore_wait(barrier, 17)
+
+    for d in range(1, 8):
+        ty, tc = yc_peer(d)
+        put(idst.at[tc * NY + ty], idbuf.at[yc], rid.at[d - 1], seq_of(ty, z, tc), x)
+    for d in range(1, 8):
+        ty, tc = yc_peer(d)
+        put(q_ref.at[tc * NY + ty], qbuf.at[yc], rq.at[d - 1], seq_of(ty, z, tc), x)
+    put(ids_ref, idxbuf.at[c], ridx.at[1], seq_of(y, z, 1 - c), x)
     for e in range(1, NX):
         for f in range(2):
             tc = lax.rem(c + f, 2)
-            put(idx_ref.at[tc], idxbuf.at[(NX - e) * 2 + c], ridx.at[(NX - e) * 2 + f],
+            put(ids_ref, idxbuf.at[(NX - e) * 2 + c], ridx.at[(NX - e) * 2 + f],
                 seq_of(y, z, tc), lax.rem(x + e, NX))
     for src, buf, sem in ((k_ref, kbuf, rk), (v_ref, vbuf, rv)):
         for d in range(1, 8):
@@ -228,6 +232,13 @@
     local[0].wait()
     local[1].wait()
     acc[...] = jnp.zeros_like(acc)
+    for k in range(3):
+        pl.semaphore_signal(zup, inc=1, device_id=(seq_of(y, lax.rem(z + 1, NZ), c), x), device_id_type=pl.DeviceIdType.MESH)
+        if k < 2:
+            pl.semaphore_signal(zdown, inc=1, device_id=(seq_of(y, lax.rem(z + NZ - 1, NZ), c), x), device_id_type=pl.DeviceIdType.MESH)
+            pl.semaphore_wait(zdown, 1)
+        pl.semaphore_wait(zup, 1)
+    w_step(1)
 
     @pl.loop(0, 8)
     def _(d):
@@ -253,18 +264,21 @@
         tz = lax.rem(z + d, NZ)
         put(msg_c.at[tz], recv_c.at[d - 1], rtc.at[d - 1], seq_of(y, tz, c), x)
         put(msg_t.at[tz], recv_t.at[d - 1], rt.at[d - 1], seq_of(y, tz, c), x)
-    w_step(1)
-
+
+    w_step(2)
     local[4].wait()
     for j in range(1, 8):
         e, f = j // 2, j % 2
         arrived(idxbuf.at[e * 2 + lax.rem(c + f, 2)], ridx.at[j])
-    for half in range(2):
-        rows = jnp.concatenate([idxbuf[e * 2 + half] for e in range(NX)], axis=0).astype(F32)
-        rows = jnp.concatenate([rows, jnp.zeros((E - 8 * NX, TOK), F32)], axis=0)
-        idcol[pl.ds(half * TOK, TOK), :] = rows.T
-
-    w_step(2)
+    idrow[...] = jnp.zeros_like(idrow)
+    for e in range(NX):
+        for dy in range(NY):
+            for part in range(2):
+                row = idxbuf[e * 2 + part, pl.ds(c * NY + lax.rem(y + dy, NY), 1), :]
+                idrow[pl.ds(e * 8 + dy, 1), pl.ds(part * TOK, TOK)] = row.astype(F32)
+    idcol[...] = idrow[...].T
+
+    w_step(3)
     total, count = msg_t[z].astype(F32), msg_c[z]
     for d in range(1, NZ):
         arrived(recv_c.at[d - 1], rtc.at[d - 1])
@@ -277,13 +291,12 @@
     for d in (4, 3, 5, 2, 6, 1, 7):
         tz = lax.rem(z + d, NZ)
         put(cent.at[z], cent.at[z], rc.at[d - 1], seq_of(y, tz, c), x)
-    w_step(3)
+    w_spread()
     local[2].wait()
     take8(kbuf, rk)
     for d in range(1, NZ):
         arrived(cent.at[lax.rem(z + NZ - d, NZ)], rc.at[d - 1])
 
-    w_spread()
     a_step(0)
     half = C // 2
     for part, dist in enumerate(((4, 3, 5, 2), (6, 1, 7, 0))):
@@ -322,6 +335,7 @@
                 put(msg_o.at[d], recv_o.at[d - 1], ro.at[d - 1], seq_of(y, tz, c), x)
 
     a_step(1)
+    w_relay()
     stats, parts = [msg_m[0]], [msg_o[0]]
     for d in range(1, NZ):
         arrived(recv_m.at[d - 1], rom.at[d - 1])
@@ -342,7 +356,6 @@
     for d in (4, 3, 5, 2, 6, 1, 7):
         tz = lax.rem(z + d, NZ)
         put(att.at[g0, z], att.at[g0, z], rz.at[d - 1], seq_of(y, tz, c), x)
-    w_relay()
     a_step(2)
     for d in range(1, NZ):
         arrived(att.at[g0, lax.rem(z + NZ - d, NZ)], rz.at[d - 1])
@@ -426,18 +439,18 @@
         pl.when(cond)(cp.wait_send)
 
 
-def chain(queries, keys, values, ids, idx, weight):
+def chain(queries, keys, values, ids, weight):
     vmem = pl.BlockSpec(memory_space=pltpu.VMEM)
     anyw = pl.BlockSpec(memory_space=pl.ANY)
     dma = pltpu.SemaphoreType.DMA
     return pl.pallas_call(
         chain_kernel,
         out_shape=jax.ShapeDtypeStruct((TOK, 8 * E), BF16),
-        in_specs=[anyw, anyw, anyw, vmem, vmem, anyw],
+        in_specs=[anyw, anyw, anyw, vmem, anyw],
         out_specs=vmem,
         scratch_shapes=[
             pltpu.VMEM((8, TOK, E), BF16), pltpu.VMEM((8, TOK, E), BF16), pltpu.VMEM((8, TOK, E), BF16),
-            pltpu.VMEM((8, 1, TOK), jnp.int32), pltpu.VMEM((8, 8, TOK), jnp.int32),
+            pltpu.VMEM((8, 1, TOK), jnp.int32), pltpu.VMEM((8, 1, TOK), jnp.int32), pltpu.VMEM((8, 8, TOK), jnp.int32),
             pltpu.VMEM((C, 2 * E), F32),
             pltpu.VMEM((NZ, BLK, E), SUM_T), pltpu.VMEM((NZ, 8, E), F32),
             pltpu.VMEM((NZ, BLK, E), OUT_T), pltpu.VMEM((NZ, 8, E), F32),
@@ -445,29 +458,25 @@
             pltpu.VMEM((NZ - 1, BLK, E), OUT_T), pltpu.VMEM((NZ - 1, 8, E), F32),
             pltpu.VMEM((NZ, BLK, E), BF16), pltpu.VMEM((8, C // 2, TOK), F32),
             pltpu.VMEM((C // 2, E), F32), pltpu.VMEM((C // 2, E), F32), pltpu.VMEM((C // 2, E), F32),
-            pltpu.VMEM((16, NZ, BLK, E), BF16), pltpu.VMEM((2 * TOK, E), F32),
+            pltpu.VMEM((16, NZ, BLK, E), BF16), pltpu.VMEM((E, 2 * TOK), F32), pltpu.VMEM((2 * TOK, E), F32),
             pltpu.VMEM((NX, NY, E, 8 * E), BF16), pltpu.VMEM((2 * TOK, 5 * E), BF16),
             pltpu.VMEM((2 * TOK, 8 * E), F32), pltpu.VMEM((TOK, 8 * E), F32),
             dma((144,)), dma((7,)), dma((7,)), dma((7,)), dma((7,)), dma((8,)),
             dma((7,)), dma((7,)), dma((7,)), dma((7,)), dma((7,)), dma((7,)),
             dma((16,)), dma((16,)), dma((4,)), dma((6,)),
             dma((16,)), dma(()), dma((4,)), dma((3,)), dma((2,)), dma((6,)), dma((6,)), dma((4,)), dma((3,)),
+            pltpu.SemaphoreType.REGULAR, pltpu.SemaphoreType.REGULAR,
         ],
         compiler_params=pltpu.CompilerParams(
             collective_id=0, has_side_effects=True, vmem_limit_bytes=48 * 1024 * 1024
         ),
         cost_estimate=pl.CostEstimate(flops=4_000_000_000, bytes_accessed=200_000_000, transcendentals=1 << 20),
-    )(queries, keys, values, ids, idx, weight)
+    )(queries, keys, values, ids, weight)
 
 
 def on_device(queries, keys, values, cluster_ids, out_weight):
-    y = lax.div(lax.axis_index("seq"), 2 * NZ)
-    ids = cluster_ids.T
-    pair = ids.reshape(2, NY, TOK)
-    pair = lax.dynamic_slice_in_dim(jnp.concatenate([pair, pair], axis=1), y, NY, axis=1)
-    idx = jnp.concatenate([pair, jnp.zeros_like(pair)], axis=1)
     q, k, v = (jnp.transpose(a, (1, 0, 2)) for a in (queries, keys, values))
-    return chain(q, k, v, ids[:, None, :], idx, out_weight)
+    return chain(q, k, v, cluster_ids.T, out_weight)
 
 
 def solution(mesh):

time: 84.4 us -> 81.7 us (0.968)
  Pallas kernels: 80.4 us -> 78.5 us
    pallas_call x1, Pallas kernels: 80.4 us -> 78.5 us  [chain(): pl.pallas_call(chain_kernel, out_shape=jax.ShapeDtypeStruct((TOK, 8 * E),...]
where the time goes in v4:
time: 81.7 us; the launch traced here: 81.5 us
  Pallas kernels  78.5 us (96%)
  local copies, waits for them, and re-layouts  3.04 us (4%)
    pallas_call x1, Pallas kernels, chain(): pl.pallas_call(chain_kernel, out_shape=jax.ShapeDtypeStruct((TOK, 8 * E),...  78.5 us
    unnamed x10, local copies, waits for them, and re-layouts  2.85 us

profile of v4, /device:TPU:1, one launch (start us, length us, event | category | flops | bytes accessed | tf_op | source)
XLA Modules:
  0.0 81.5 jit_solution(12316800469236410722)
XLA Ops:
  0.0 0.0 copy-start.2
  0.0 0.0 copy-start.3
  0.0 1.2 %copy.12 = bf16[256,8,128]{2,0,1:T(8,128)(2,1)S(1)} copy(bf16[256,8,128]{2,1,0:T(8,128)(2,1)} %param.5) | data formatting | bytes 1048576 | tf_op args[0]
  1.2 0.0 copy-done.2
  1.2 0.1 copy-done.3
  1.4 0.0 copy-start
  1.4 0.0 copy-start.1
  1.4 0.2 copy_bitcast_fusion
  1.6 0.7 copy-done
  2.3 0.0 copy-done.1
  2.3 78.5 %shard_map.55 = bf16[256,1024]{1,0:T(8,128)(2,1)S(1)} custom-call(bf16[8,256,128]{2,1,0:T(8,128)(2,1)S(1)} %bitcast.8, bf16[8,256,128]{2,1,0:T(8,128)(2,1)S(1)} %get-tuple-element.6.k_ref, bf16[8,256,128]{2,1,0:T(8,128)(2,1)S(1)} %get-tuple-element.5.v_ref, s32[8,256]{1,0:T(8,128)S(1)} %bitcast.9, bf16[64,1024]{1,0:T(8,128)(2,1)S(1)} %copy-done), custom_call_target="tpu_custom_call" | custom-call | flops 4000000000 | bytes 200000000 | tf_op jit(solution)/shard_map/pallas_call | solution.py:446
  80.7 0.8 copy.14
Async XLA Ops:
  0.0 1.2 %copy-start.2 = (bf16[256,8,128]{2,1,0:T(8,128)(2,1)S(1)}, bf16[256,8,128]{2,1,0:T(8,128)(2,1)}, u32[]{:S(2)}) copy-start(bf16[256,8,128]{2,1,0:T(8,128)(2,1)} %param.7) | copy-start | bytes 1572868
  0.0 1.4 %copy-start.3 = (bf16[256,8,128]{2,1,0:T(8,128)(2,1)S(1)}, bf16[256,8,128]{2,1,0:T(8,128)(2,1)}, u32[]{:S(2)}) copy-start(bf16[256,8,128]{2,1,0:T(8,128)(2,1)} %param.6) | copy-start | bytes 1572868
  1.4 0.9 %copy-start = (bf16[64,1024]{1,0:T(8,128)(2,1)S(1)}, bf16[64,1024]{1,0:T(8,128)(2,1)}, u32[]{:S(2)}) copy-start(bf16[64,1024]{1,0:T(8,128)(2,1)} %w_ref.1) | copy-start | bytes 393220
  1.4 0.9 %copy-start.1 = (s32[256,8]{0,1:T(8,128)S(1)}, s32[256,8]{0,1:T(8,128)}, u32[]{:S(2)}) copy-start(s32[256,8]{0,1:T(8,128)} %param.8) | copy-start | bytes 24580

commit v5 on v4

--- a/solution.py
+++ b/solution.py
@@ -15,14 +15,14 @@
 HALF = E // 2
 EXP2_SCALE = math.log2(math.e) / math.sqrt(E)
 F32, BF16 = jnp.float32, jnp.bfloat16
-SIDE = 256
-SUM_T, OUT_T = BF16, BF16
+SIDE = 384
+SUM_T, OUT_T, PAIR_T = BF16, BF16, BF16
 
 
 def chain_kernel(
     q_ref, k_ref, v_ref, ids_ref, w_ref, out_ref,
     qbuf, kbuf, vbuf, idst, idbuf, idxbuf, acc, msg_t, msg_c, msg_o, msg_m, recv_t, recv_c, recv_o, recv_m, cent, sbuf, mx, ls, oacc,
-    att, idrow, idcol, wbuf, feat, psum, other,
+    att, idrow, idcol, wbuf, feat, psum, give, other,
     ssem, rq, rk, rv, rid, ridx, rt, rtc, rc, ro, rom, rz, ra, rb, rf, lsem, swc, rwo, rw1, rwr, rwl, rwy, rwa, rwra, rwla, zup, zdown,
 ):
     s_id, x = lax.axis_index("seq"), lax.axis_index("head")
@@ -239,6 +239,7 @@
             pl.semaphore_wait(zdown, 1)
         pl.semaphore_wait(zup, 1)
     w_step(1)
+    w_step(2)
 
     @pl.loop(0, 8)
     def _(d):
@@ -265,7 +266,7 @@
         put(msg_c.at[tz], recv_c.at[d - 1], rtc.at[d - 1], seq_of(y, tz, c), x)
         put(msg_t.at[tz], recv_t.at[d - 1], rt.at[d - 1], seq_of(y, tz, c), x)
 
-    w_step(2)
+    w_step(3)
     local[4].wait()
     for j in range(1, 8):
         e, f = j // 2, j % 2
@@ -278,7 +279,6 @@
                 idrow[pl.ds(e * 8 + dy, 1), pl.ds(part * TOK, TOK)] = row.astype(F32)
     idcol[...] = idrow[...].T
 
-    w_step(3)
     total, count = msg_t[z].astype(F32), msg_c[z]
     for d in range(1, NZ):
         arrived(recv_c.at[d - 1], rtc.at[d - 1])
@@ -334,8 +334,8 @@
                 put(msg_m.at[d], recv_m.at[d - 1], rom.at[d - 1], seq_of(y, tz, c), x)
                 put(msg_o.at[d], recv_o.at[d - 1], ro.at[d - 1], seq_of(y, tz, c), x)
 
+    w_relay()
     a_step(1)
-    w_relay()
     stats, parts = [msg_m[0]], [msg_o[0]]
     for d in range(1, NZ):
         arrived(recv_m.at[d - 1], rom.at[d - 1])
@@ -360,7 +360,6 @@
     for d in range(1, NZ):
         arrived(att.at[g0, lax.rem(z + NZ - d, NZ)], rz.at[d - 1])
 
-    a_step(3)
     low, high = pl.ds(0, NZ // 2), pl.ds(NZ // 2, NZ // 2)
 
     def g_of(dx, dy):
@@ -380,6 +379,7 @@
     to_x(g0, high, rb, 0)
     to_x(g0, low, ra, 0)
     to_y(g0, high, rb, 0)
+    a_step(3)
     for e in range(1, NY):
         arrived(att.at[g_of(0, e), low], ra.at[e])
         to_x(g_of(0, e), low, ra, e)
@@ -388,8 +388,7 @@
 
     lanes = lax.broadcasted_iota(jnp.int32, (2 * TOK, C), 1).astype(F32)
     groups = (
-        ((0, 0), (0, 1), (0, 2), (0, 3)),
-        ((1, 0), (2, 0), (3, 0)),
+        ((0, 0), (0, 1), (0, 2), (0, 3), (1, 0), (2, 0), (3, 0)),
         ((1, 1), (1, 2), (2, 1), (2, 2)),
         ((1, 3), (3, 1), (2, 3), (3, 2), (3, 3)),
     )
@@ -426,13 +425,13 @@
         else:
             for n in range(NX):
                 cols = pl.ds(n * TOK, TOK)
-                psum[theirs, cols] += term(theirs, cols)
-                put(psum.at[theirs, cols], other.at[:, cols], rf.at[n], seq_of(y, z, 1 - c), x)
+                give[:, cols] = (psum[theirs, cols] + term(theirs, cols)).astype(PAIR_T)
+                put(give.at[:, cols], other.at[:, cols], rf.at[n], seq_of(y, z, 1 - c), x)
             for n in range(NX):
                 cols = pl.ds(n * TOK, TOK)
                 total = psum[mine, cols] + term(mine, cols)
                 arrived(other.at[:, cols], rf.at[n])
-                out_ref[:, cols] = (total + other[:, cols]).astype(BF16)
+                out_ref[:, cols] = (total + other[:, cols].astype(F32)).astype(BF16)
     for cp in sends:
         cp.wait_send()
     for cond, cp in maybe:
@@ -459,8 +458,9 @@
             pltpu.VMEM((NZ, BLK, E), BF16), pltpu.VMEM((8, C // 2, TOK), F32),
             pltpu.VMEM((C // 2, E), F32), pltpu.VMEM((C // 2, E), F32), pltpu.VMEM((C // 2, E), F32),
             pltpu.VMEM((16, NZ, BLK, E), BF16), pltpu.VMEM((E, 2 * TOK), F32), pltpu.VMEM((2 * TOK, E), F32),
-            pltpu.VMEM((NX, NY, E, 8 * E), BF16), pltpu.VMEM((2 * TOK, 5 * E), BF16),
-            pltpu.VMEM((2 * TOK, 8 * E), F32), pltpu.VMEM((TOK, 8 * E), F32),
+            pltpu.VMEM((NX, NY, E, 8 * E), BF16), pltpu.VMEM((2 * TOK, 16 * E), BF16),
+            pltpu.VMEM((2 * TOK, 8 * E), F32), pltpu.VMEM((TOK, 8 * E), PAIR_T),
+            pltpu.VMEM((TOK, 8 * E), PAIR_T),
             dma((144,)), dma((7,)), dma((7,)), dma((7,)), dma((7,)), dma((8,)),
             dma((7,)), dma((7,)), dma((7,)), dma((7,)), dma((7,)), dma((7,)),
             dma((16,)), dma((16,)), dma((4,)), dma((6,)),

time: 81.7 us -> 79.2 us (0.969)
  Pallas kernels: 78.5 us -> 76 us
    pallas_call x1, Pallas kernels: 78.5 us -> 76 us  [chain(): pl.pallas_call(chain_kernel, out_shape=jax.ShapeDtypeStruct((TOK, 8 * E),...]
where the time goes in v5:
time: 79.2 us; the launch traced here: 79 us
  Pallas kernels  76 us (96%)
  local copies, waits for them, and re-layouts  3.04 us (4%)
    pallas_call x1, Pallas kernels, chain(): pl.pallas_call(chain_kernel, out_shape=jax.ShapeDtypeStruct((TOK, 8 * E),...  76 us
    unnamed x10, local copies, waits for them, and re-layouts  2.85 us

profile of v5, /device:TPU:1, one launch (start us, length us, event | category | flops | bytes accessed | tf_op | source)
XLA Modules:
  0.0 79.0 jit_solution(14138555823358246551)
XLA Ops:
  0.0 0.0 copy-start.2
  0.0 0.0 copy-start.3
  0.0 1.2 %copy.12 = bf16[256,8,128]{2,0,1:T(8,128)(2,1)S(1)} copy(bf16[256,8,128]{2,1,0:T(8,128)(2,1)} %param.5) | data formatting | bytes 1048576 | tf_op args[0]
  1.2 0.0 copy-done.2
  1.2 0.1 copy-done.3
  1.4 0.0 copy-start
  1.4 0.0 copy-start.1
  1.4 0.2 copy_bitcast_fusion
  1.6 0.7 copy-done
  2.3 0.0 copy-done.1
  2.3 76.0 %shard_map.55 = bf16[256,1024]{1,0:T(8,128)(2,1)S(1)} custom-call(bf16[8,256,128]{2,1,0:T(8,128)(2,1)S(1)} %bitcast.8, bf16[8,256,128]{2,1,0:T(8,128)(2,1)S(1)} %get-tuple-element.6.k_ref, bf16[8,256,128]{2,1,0:T(8,128)(2,1)S(1)} %get-tuple-element.5.v_ref, s32[8,256]{1,0:T(8,128)S(1)} %bitcast.9, bf16[64,1024]{1,0:T(8,128)(2,1)S(1)} %copy-done), custom_call_target="tpu_custom_call" | custom-call | flops 4000000000 | bytes 200000000 | tf_op jit(solution)/shard_map/pallas_call | solution.py:445
  78.2 0.8 %copy.14 = bf16[256,1024]{1,0:T(8,128)(2,1)} copy(bf16[256,1024]{1,0:T(8,128)(2,1)S(1)} %shard_map.55) | data formatting | bytes 1048576
Async XLA Ops:
  0.0 1.2 %copy-start.2 = (bf16[256,8,128]{2,1,0:T(8,128)(2,1)S(1)}, bf16[256,8,128]{2,1,0:T(8,128)(2,1)}, u32[]{:S(2)}) copy-start(bf16[256,8,128]{2,1,0:T(8,128)(2,1)} %param.7) | copy-start | bytes 1572868
  0.0 1.4 %copy-start.3 = (bf16[256,8,128]{2,1,0:T(8,128)(2,1)S(1)}, bf16[256,8,128]{2,1,0:T(8,128)(2,1)}, u32[]{:S(2)}) copy-start(bf16[256,8,128]{2,1,0:T(8,128)(2,1)} %param.6) | copy-start | bytes 1572868
  1.4 0.9 %copy-start = (bf16[64,1024]{1,0:T(8,128)(2,1)S(1)}, bf16[64,1024]{1,0:T(8,128)(2,1)}, u32[]{:S(2)}) copy-start(bf16[64,1024]{1,0:T(8,128)(2,1)} %w_ref.1) | copy-start | bytes 393220
  1.4 0.9 %copy-start.1 = (s32[256,8]{0,1:T(8,128)S(1)}, s32[256,8]{0,1:T(8,128)}, u32[]{:S(2)}) copy-start(s32[256,8]{0,1:T(8,128)} %param.8) | copy-start | bytes 24580

commit v6 on v5

--- a/solution.py
+++ b/solution.py
@@ -366,12 +366,12 @@
         return lax.rem(x + dx, NX) * NY + lax.rem(y + dy, NY)
 
     def to_y(g, part, sem, dx):
-        for e in range(1, NY):
+        for e in (2, 1, 3):
             put(att.at[g, part], att.at[g, part], sem.at[dx * NY + NY - e],
                 seq_of(lax.rem(y + e, NY), z, c), x)
 
     def to_x(g, part, sem, dy):
-        for e in range(1, NX):
+        for e in (2, 1, 3):
             put(att.at[g, part], att.at[g, part], sem.at[(NX - e) * NY + dy],
                 s_id, lax.rem(x + e, NX))
 

time: 79.2 us -> 79 us (level)
  no operation moved by 1% of the time
where the time goes in v6:
time: 79 us; the launch traced here: 78.9 us
  Pallas kernels  75.8 us (96%)
  local copies, waits for them, and re-layouts  3.04 us (4%)
    pallas_call x1, Pallas kernels, chain(): pl.pallas_call(chain_kernel, out_shape=jax.ShapeDtypeStruct((TOK, 8 * E),...  75.8 us
    unnamed x10, local copies, waits for them, and re-layouts  2.85 us

profile of v6, /device:TPU:1, one launch (start us, length us, event | category | flops | bytes accessed | tf_op | source)
XLA Modules:
  0.0 78.9 jit_solution(12813637852772408373)
XLA Ops:
  0.0 0.0 copy-start.2
  0.0 0.0 copy-start.3
  0.0 1.2 %copy.12 = bf16[256,8,128]{2,0,1:T(8,128)(2,1)S(1)} copy(bf16[256,8,128]{2,1,0:T(8,128)(2,1)} %param.5) | data formatting | bytes 1048576 | tf_op args[0]
  1.2 0.0 copy-done.2
  1.2 0.1 copy-done.3
  1.4 0.0 copy-start
  1.4 0.0 copy-start.1
  1.4 0.2 copy_bitcast_fusion
  1.6 0.7 copy-done
  2.3 0.0 copy-done.1
  2.3 75.8 %shard_map.55 = bf16[256,1024]{1,0:T(8,128)(2,1)S(1)} custom-call(bf16[8,256,128]{2,1,0:T(8,128)(2,1)S(1)} %bitcast.8, bf16[8,256,128]{2,1,0:T(8,128)(2,1)S(1)} %get-tuple-element.6.k_ref, bf16[8,256,128]{2,1,0:T(8,128)(2,1)S(1)} %get-tuple-element.5.v_ref, s32[8,256]{1,0:T(8,128)S(1)} %bitcast.9, bf16[64,1024]{1,0:T(8,128)(2,1)S(1)} %copy-done), custom_call_target="tpu_custom_call" | custom-call | flops 4000000000 | bytes 200000000 | tf_op jit(solution)/shard_map/pallas_call | solution.py:445
  78.1 0.8 %copy.14 = bf16[256,1024]{1,0:T(8,128)(2,1)} copy(bf16[256,1024]{1,0:T(8,128)(2,1)S(1)} %shard_map.55) | data formatting | bytes 1048576
Async XLA Ops:
  0.0 1.2 %copy-start.2 = (bf16[256,8,128]{2,1,0:T(8,128)(2,1)S(1)}, bf16[256,8,128]{2,1,0:T(8,128)(2,1)}, u32[]{:S(2)}) copy-start(bf16[256,8,128]{2,1,0:T(8,128)(2,1)} %param.7) | copy-start | bytes 1572868
  0.0 1.4 %copy-start.3 = (bf16[256,8,128]{2,1,0:T(8,128)(2,1)S(1)}, bf16[256,8,128]{2,1,0:T(8,128)(2,1)}, u32[]{:S(2)}) copy-start(bf16[256,8,128]{2,1,0:T(8,128)(2,1)} %param.6) | copy-start | bytes 1572868
  1.4 0.9 %copy-start = (bf16[64,1024]{1,0:T(8,128)(2,1)S(1)}, bf16[64,1024]{1,0:T(8,128)(2,1)}, u32[]{:S(2)}) copy-start(bf16[64,1024]{1,0:T(8,128)(2,1)} %w_ref.1) | copy-start | bytes 393220
  1.4 0.9 %copy-start.1 = (s32[256,8]{0,1:T(8,128)S(1)}, s32[256,8]{0,1:T(8,128)}, u32[]{:S(2)}) copy-start(s32[256,8]{0,1:T(8,128)} %param.8) | copy-start | bytes 24580
